TPU v7x, 32 devices: a whole 2x2x4 slice. The times are simulated.
32 devices in a mesh: grp: 2 (over y), tm: 4 (over z), row: 2 (over x), col: 2 (over core).
Axes of the slice: x: 2, y: 2, z: 4, core: 2. Of those that a mesh axis runs over, the one named last changes fastest.
Arguments:
- frames: bfloat16 [8, 16, 9216], P(('grp', 'tm'), 'row', 'col'), parts along dimension 0, may hold values from -6 to 6
- owner_map: int32 [8], P('grp'), parts along dimension 0, may hold values from 0 to 3, each once
- valid_blocks: int32 [8, 2, 36], P(('grp', 'tm'), 'row', 'col'), parts along dimension 0, may hold values 0 or 1
- deblock_weight: bfloat16 [288, 32], replicated, may hold values from -0.375 to 0.375
- deblock_bias: float32 [32], replicated, may hold values from -3 to 3
- encoder_weight: bfloat16 [864, 64], replicated, may hold values from -0.21875 to 0.21875
- encoder_bias: float32 [64], replicated, may hold values from -3 to 3
Outputs:
- encoded: bfloat16 [6, 2, 4, 9216], P('grp', 'row', 'tm', 'col'), parts along dimension 0
There are 2 independent parts, one for each index of `grp`. A program takes and returns all parts, laid end to end along the dimension named above; an argument that names none is the same for every part. Nothing has to cross between parts.
Inputs may be any that keep to these rules, and one draw needn't show every extreme that they name: `owner_map`: each time index is held by exactly one slot.
All inputs are finite; a program needn't handle non-finite values. No bound on the sum of `valid_blocks` on one device may be relied on, other than what follows from the above.
Results may differ from a plain program's by a relative error of at most 0.0085.
Values may be sent and summed in bfloat16 or wider, within the bound.
No kernel may reach another device: no remote copies, remote signals or barrier semaphores. Data moves between devices by JAX's collectives and lax.ppermute only.
A program may use at most 64 MiB of HBM per device.

v0:
```python
import jax
import jax.numpy as jnp
from jax import lax
from jax.sharding import PartitionSpec as P

CH = 32
OUTC = 64


def extended(cells, sides, width):
    for axis, dim in sides:
        count = lax.axis_size(axis)
        ends = count - 1
        head = lax.slice_in_dim(cells, 0, width, axis=dim)
        tail = lax.slice_in_dim(cells, cells.shape[dim] - width, cells.shape[dim], axis=dim)
        cells = jnp.concatenate(
            [
                lax.ppermute(tail, axis, [(i, (i + 1) % count) for i in range(ends)]),
                cells,
                lax.ppermute(head, axis, [((i + 1) % count, i) for i in range(ends)]),
            ],
            axis=dim,
        )
    return cells


def conv_taps(padded, weight, height, extent):
    channels = padded.shape[-1]
    summed = jnp.zeros((), jnp.float32)
    for row_step in range(3):
        stripe = padded[..., row_step : row_step + height, :, :]
        patches = jnp.concatenate(
            [stripe[..., col_step : col_step + extent, :] for col_step in range(3)], axis=-1
        )
        patches = patches.reshape(-1, 3 * channels)
        kernel = weight[row_step * 3 * channels : (row_step + 1) * 3 * channels]
        summed = summed + jnp.dot(patches, kernel, preferred_element_type=jnp.float32)
    return summed


def pool_pairs(source):
    leading = source.shape[:-3]
    height, extent, channels = source.shape[-3:]
    grouped = source.astype(jnp.float32).reshape(
        leading + (height // 2, 2, extent // 2, 2, channels)
    )
    depth = len(leading)
    return jnp.mean(grouped, axis=(depth + 1, depth + 3)).astype(jnp.bfloat16)


def regroup(stacked):
    return lax.all_to_all(stacked, "tm", split_axis=0, concat_axis=0, tiled=True)


def on_device(
    frames, owner_map, valid_blocks, deblock_weight, deblock_bias, encoder_weight, encoder_bias
):
    height = frames.shape[1]
    extent = frames.shape[2] // CH
    image = frames.reshape(height, extent, CH)
    framed = extended(image, (("row", 0), ("col", 1)), 1)
    filtered = (
        conv_taps(framed, deblock_weight, height, extent).reshape(height, extent, CH) + deblock_bias
    )
    blocks = valid_blocks[0].astype(jnp.float32)
    coverage = jnp.broadcast_to(blocks[:, None, :, None], (height // 8, 8, extent // 8, 8)).reshape(
        height, extent, 1
    )
    cleaned = (image.astype(jnp.float32) + coverage * filtered).astype(jnp.bfloat16)
    bands = lax.axis_size("tm")
    source = pool_pairs(cleaned)
    source_rows = source.shape[0]
    source_cols = source.shape[1]
    stride = source_rows // bands
    wide = extended(source, (("row", 0), ("col", 1)), 1)
    span = source_cols + 2
    upper = wide[:source_rows].reshape(bands, stride, span, CH)
    middle = wide[1 : 1 + source_rows].reshape(bands, stride, span, CH)
    lower = wide[2 : 2 + source_rows].reshape(bands, stride, span, CH)
    stacked = jnp.concatenate([upper, middle, lower], axis=1)
    arrived = regroup(stacked.reshape(bands, stride + 2, span * CH))
    ready = arrived.reshape(bands, stride + 2, span, CH)
    indices = jnp.arange(bands, dtype=jnp.int32)
    matches = (owner_map[None, :] == indices[:, None]).astype(jnp.int32)
    slot_of_time = jnp.sum(matches * indices[None, :], axis=1)
    ordered = jnp.take(ready, slot_of_time, axis=0)
    band_rows = ordered.shape[1] - 2
    band_cols = ordered.shape[2] - 2
    current = ordered[1:]
    previous = ordered[:-1]
    earlier = jnp.concatenate([ordered[:1], ordered[:-2]], axis=0)
    summed = encoder_bias
    for frame_lag, history in enumerate((current, previous, earlier)):
        kernel = encoder_weight[frame_lag * 9 * CH : (frame_lag + 1) * 9 * CH]
        summed = summed + conv_taps(history, kernel, band_rows, band_cols)
    encoded = summed.astype(jnp.bfloat16)
    return encoded.reshape(bands - 1, 1, band_rows, band_cols * OUTC)


def solution(mesh):
    return jax.shard_map(
        on_device,
        mesh=mesh,
        in_specs=(
            P(("grp", "tm"), "row", "col"),
            P("grp"),
            P(("grp", "tm"), "row", "col"),
            P(),
            P(),
            P(),
            P(),
        ),
        out_specs=P("grp", "row", "tm", "col"),
        check_vma=False,
    )
```

profile of v0, /device:TPU:0, one launch (start us, length us, event | category | flops | bytes accessed | tf_op | source)
XLA Modules:
  0.0 53.4 jit_solution(6096664387549325175)
XLA Ops:
  0.0 1.1 %slice_reduce_fusion = (bf16[4608]{0:T(1024)(128)(2,1)S(1)}, bf16[4608]{0:T(1024)(128)(2,1)S(1)}) fusion(bf16[1,8,4608]{2,1,0:T(8,128)(2,1)} %param.7), kind=kLoop, calls=%fused_computation.68 | loop fusion | bytes 36864 | tf_op jit(solution)/shard_map/slice | solution.py:14
  1.2 4.9 %collective-permute-start = (bf16[1,144,32]{2,1,0:T(8,128)(2,1)S(1)}, bf16[1,144,32]{2,1,0:T(8,128)(2,1)S(1)}, u32[]{:S(2)}, u32[]{:S(2)}) collective-permute-start(bf16[1,144,32]{2,1,0:T(8,128)(2,1)S(1)} %slice.267), channel_id=1, source_target_pairs={{0,2},{1,3},{4,6},{5,7},{8,10},{9,11},{12,14},{13,15},{16,18},{17,... | collective-permute-start | bytes 27656 | tf_op jit(solution)/shard_map/ppermute | solution.py:18
  6.2 1.3 %collective-permute-start.1 = (bf16[1,144,32]{2,1,0:T(8,128)(2,1)S(1)}, bf16[1,144,32]{2,1,0:T(8,128)(2,1)S(1)}, u32[]{:S(2)}, u32[]{:S(2)}) collective-permute-start(bf16[1,144,32]{2,1,0:T(8,128)(2,1)S(1)} %slice.269), channel_id=1, source_target_pairs={{2,0},{3,1},{6,4},{7,5},{10,8},{11,9},{14,12},{15,13},{18,16},{19,... | collective-permute-start | bytes 27656 | tf_op jit(solution)/shard_map/ppermute | solution.py:20
  7.9 4.1 %collective-permute-done.1 = bf16[1,144,32]{2,1,0:T(8,128)(2,1)S(1)} collective-permute-done((bf16[1,144,32]{2,1,0:T(8,128)(2,1)S(1)}, bf16[1,144,32]{2,1,0:T(8,128)(2,1)S(1)}, u32[]{:S(2)}, u32[]{:S(2)}) %collective-permute-start.1) | collective-permute-done | bytes 9248 | tf_op jit(solution)/shard_map/ppermute | solution.py:20
  12.3 1.3 %collective-permute-start.2 = (bf16[10,1,32]{1,2,0:T(8,128)(2,1)S(1)}, bf16[10,1,32]{1,2,0:T(8,128)(2,1)S(1)}, u32[]{:S(2)}, u32[]{:S(2)}) collective-permute-start(bf16[10,1,32]{1,2,0:T(8,128)(2,1)S(1)} %get-tuple-element.33), channel_id=1, source_target_pairs={{0,1},{2,3},{4,5},{6,7},{8,9},{10,11},{12,13},{14,15},{16,17},{18,... | collective-permute-start | bytes 1928 | tf_op jit(solution)/shard_map/ppermute | solution.py:18
  13.6 1.3 %collective-permute-start.3 = (bf16[10,1,32]{1,2,0:T(8,128)(2,1)S(1)}, bf16[10,1,32]{1,2,0:T(8,128)(2,1)S(1)}, u32[]{:S(2)}, u32[]{:S(2)}) collective-permute-start(bf16[10,1,32]{1,2,0:T(8,128)(2,1)S(1)} %get-tuple-element.34), channel_id=1, source_target_pairs={{1,0},{3,2},{5,4},{7,6},{9,8},{11,10},{13,12},{15,14},{17,16},{19,... | collective-permute-start | bytes 1928 | tf_op jit(solution)/shard_map/ppermute | solution.py:20
  15.9 0.9 %collective-permute-done.3 = bf16[10,1,32]{1,2,0:T(8,128)(2,1)S(1)} collective-permute-done((bf16[10,1,32]{1,2,0:T(8,128)(2,1)S(1)}, bf16[10,1,32]{1,2,0:T(8,128)(2,1)S(1)}, u32[]{:S(2)}, u32[]{:S(2)}) %collective-permute-start.3) | collective-permute-done | bytes 672 | tf_op jit(solution)/shard_map/ppermute | solution.py:20
  19.8 0.7 %copy-done.4 = f32[32]{0:T(128)S(1)} copy-done((f32[32]{0:T(128)S(1)}, f32[32]{0:T(128)}, u32[]{:S(2)}) %copy-start.4) | copy-done | bytes 152
  20.5 0.7 %convert_reduce_fusion = f32[4,72,32]{2,1,0:T(8,128)S(1)} fusion(f32[4,2,72,2,32]{4,3,2,1,0:T(2,128)S(1)} %reshape.135, f32[4,2,72,2,32]{4,3,2,1,0:T(2,128)S(1)} %bitcast.33, f32[32]{0:T(128)S(1)} %copy-done.4, f32[72]{0:T(128)S(1)} %broadcast_in_dim.25), kind=kLoop, calls=%fused_computation.13 | loop fusion | flops 211968 | bytes 332192 | tf_op jit(solution)/shard_map/reduce_sum | solution.py:48
  21.2 1.6 %collective-permute-start.4 = (bf16[1,72,32]{2,1,0:T(8,128)(2,1)S(1)}, bf16[1,72,32]{2,1,0:T(8,128)(2,1)S(1)}, u32[]{:S(2)}, u32[]{:S(2)}) collective-permute-start(bf16[1,72,32]{2,1,0:T(8,128)(2,1)S(1)} %get-tuple-element.45), channel_id=1, source_target_pairs={{0,2},{1,3},{4,6},{5,7},{8,10},{9,11},{12,14},{13,15},{16,18},{17,... | collective-permute-start | bytes 13832 | tf_op jit(solution)/shard_map/ppermute | solution.py:18
  22.9 1.3 %collective-permute-start.5 = (bf16[1,72,32]{2,1,0:T(8,128)(2,1)S(1)}, bf16[1,72,32]{2,1,0:T(8,128)(2,1)S(1)}, u32[]{:S(2)}, u32[]{:S(2)}) collective-permute-start(bf16[1,72,32]{2,1,0:T(8,128)(2,1)S(1)} %get-tuple-element.46), channel_id=1, source_target_pairs={{2,0},{3,1},{6,4},{7,5},{10,8},{11,9},{14,12},{15,13},{18,16},{19,... | collective-permute-start | bytes 13832 | tf_op jit(solution)/shard_map/ppermute | solution.py:20
  24.4 4.1 %collective-permute-done.5 = bf16[1,72,32]{2,1,0:T(8,128)(2,1)S(1)} collective-permute-done((bf16[1,72,32]{2,1,0:T(8,128)(2,1)S(1)}, bf16[1,72,32]{2,1,0:T(8,128)(2,1)S(1)}, u32[]{:S(2)}, u32[]{:S(2)}) %collective-permute-start.5) | collective-permute-done | bytes 4640 | tf_op jit(solution)/shard_map/ppermute | solution.py:20
  28.7 1.3 %collective-permute-start.6 = (bf16[6,1,32]{1,2,0:T(8,128)(2,1)S(1)}, bf16[6,1,32]{1,2,0:T(8,128)(2,1)S(1)}, u32[]{:S(2)}, u32[]{:S(2)}) collective-permute-start(bf16[6,1,32]{1,2,0:T(8,128)(2,1)S(1)} %get-tuple-element.50), channel_id=1, source_target_pairs={{0,1},{2,3},{4,5},{6,7},{8,9},{10,11},{12,13},{14,15},{16,17},{18,... | collective-permute-start | bytes 1160 | tf_op jit(solution)/shard_map/ppermute | solution.py:18
  30.0 1.3 %collective-permute-start.7 = (bf16[6,1,32]{1,2,0:T(8,128)(2,1)S(1)}, bf16[6,1,32]{1,2,0:T(8,128)(2,1)S(1)}, u32[]{:S(2)}, u32[]{:S(2)}) collective-permute-start(bf16[6,1,32]{1,2,0:T(8,128)(2,1)S(1)} %get-tuple-element.51), channel_id=1, source_target_pairs={{1,0},{3,2},{5,4},{7,6},{9,8},{11,10},{13,12},{15,14},{17,16},{19,... | collective-permute-start | bytes 1160 | tf_op jit(solution)/shard_map/ppermute | solution.py:20
  31.3 1.8 %collective-permute-done.7 = bf16[6,1,32]{1,2,0:T(8,128)(2,1)S(1)} collective-permute-done((bf16[6,1,32]{1,2,0:T(8,128)(2,1)S(1)}, bf16[6,1,32]{1,2,0:T(8,128)(2,1)S(1)}, u32[]{:S(2)}, u32[]{:S(2)}) %collective-permute-start.7) | collective-permute-done | bytes 416 | tf_op jit(solution)/shard_map/ppermute | solution.py:20
  34.1 0.7 %copy.96 = bf16[4,3,2368]{2,1,0:T(4,128)(2,1)} copy(bf16[4,3,2368]{2,0,1:T(4,128)(2,1)S(1)} %pad_maximum_fusion.7) | data formatting | bytes 113664 | tf_op jit(solution)/shard_map/concatenate | solution.py:80
  34.8 4.9 %all-to-all-start = ((bf16[4,3,2368]{2,1,0:T(4,128)(2,1)}), bf16[4,3,2368]{2,1,0:T(4,128)(2,1)S(1)}, u32[]{:S(2)}, u32[]{:S(2)}) async-start(bf16[4,3,2368]{2,1,0:T(4,128)(2,1)} %copy.96), calls=%async_computation | async-start | bytes 155648 | tf_op jit(solution)/shard_map/all_to_all | solution.py:52
  39.7 5.8 %all-to-all-done = bf16[4,3,2368]{2,1,0:T(4,128)(2,1)S(1)} async-done(((bf16[4,3,2368]{2,1,0:T(4,128)(2,1)}), bf16[4,3,2368]{2,1,0:T(4,128)(2,1)S(1)}, u32[]{:S(2)}, u32[]{:S(2)}) %all-to-all-start) | async-done | bytes 56864 | tf_op jit(solution)/shard_map/all_to_all | solution.py:52
  45.7 0.6 %gather_fusion = bf16[4,3,74,32]{3,2,1,0:T(8,128)(2,1)S(1)} fusion(bf16[4,3,74,32]{3,2,0,1:T(8,128)(2,1)S(1)} %reshape.124, s32[1024]{0:T(1024)S(1)} %pad_clamp_fusion), kind=kCustom, calls=%fused_computation | custom fusion | bytes 113680 | tf_op jit(solution)/shard_map/jit(_take)/gather | solution.py:86
  46.4 0.7 %copy-done = bf16[4,3,74,32]{3,2,1,0:T(8,128)(2,1)} copy-done((bf16[4,3,74,32]{3,2,1,0:T(8,128)(2,1)}, bf16[4,3,74,32]{3,2,1,0:T(8,128)(2,1)S(1)}, u32[]{:S(2)}) %copy-start) | copy-done | bytes 56856
  47.3 0.7 %slice-done = bf16[1,3,74,32]{3,2,1,0:T(8,128)(2,1)S(1)} async-done(((bf16[4,3,74,32]{3,2,1,0:T(8,128)(2,1)}), bf16[1,3,74,32]{3,2,1,0:T(8,128)(2,1)S(1)}, s32[]{:S(2)}) %slice-start) | async-done | bytes 14232 | tf_op jit(solution)/shard_map/slice | solution.py:91
  48.7 0.8 %copy-done.2 = bf16[864,64]{0,1:T(8,128)(2,1)S(1)} copy-done((bf16[864,64]{0,1:T(8,128)(2,1)S(1)}, bf16[864,64]{0,1:T(8,128)(2,1)}, u32[]{:S(2)}) %copy-start.2) | copy-done | bytes 110616
  51.3 0.6 %copy-done.5 = f32[64]{0:T(128)S(1)} copy-done((f32[64]{0:T(128)S(1)}, f32[64]{0:T(128)}, u32[]{:S(2)}) %copy-start.5) | copy-done | bytes 280
  52.7 0.7 %reshape.134 = bf16[3,1,1,4608]{3,0,2,1:T(4,128)(2,1)} reshape(bf16[216,64]{1,0:T(8,128)(2,1)S(1)} %copy.103) | data formatting | bytes 55296 | tf_op jit(solution)/shard_map/reshape | solution.py:97
  (91 shorter events, 9.9 us)
Async XLA Ops:
  0.0 7.5 %copy-start.1 = (bf16[1,8,4608]{2,1,0:T(8,128)(2,1)S(1)}, bf16[1,8,4608]{2,1,0:T(8,128)(2,1)}, u32[]{:S(2)}) copy-start(bf16[1,8,4608]{2,1,0:T(8,128)(2,1)} %param.7) | copy-start | bytes 221188
  1.2 6.7 %collective-permute-start = (bf16[1,144,32]{2,1,0:T(8,128)(2,1)S(1)}, bf16[1,144,32]{2,1,0:T(8,128)(2,1)S(1)}, u32[]{:S(2)}, u32[]{:S(2)}) collective-permute-start(bf16[1,144,32]{2,1,0:T(8,128)(2,1)S(1)} %slice.267), channel_id=1, source_target_pairs={{0,2},{1,3},{4,6},{5,7},{8,10},{9,11},{12,14},{13,15},{16,18},{17,... | collective-permute-start | bytes 27656 | tf_op jit(solution)/shard_map/ppermute | solution.py:18
  6.1 1.4 %copy-start.6 = (s32[1,1,18]{2,1,0:T(1,128)S(1)}, s32[1,1,18]{2,1,0:T(1,128)}, u32[]{:S(2)}) copy-start(s32[1,1,18]{2,1,0:T(1,128)} %param.9) | copy-start | bytes 220
  6.2 5.9 %collective-permute-start.1 = (bf16[1,144,32]{2,1,0:T(8,128)(2,1)S(1)}, bf16[1,144,32]{2,1,0:T(8,128)(2,1)S(1)}, u32[]{:S(2)}, u32[]{:S(2)}) collective-permute-start(bf16[1,144,32]{2,1,0:T(8,128)(2,1)S(1)} %slice.269), channel_id=1, source_target_pairs={{2,0},{3,1},{6,4},{7,5},{10,8},{11,9},{14,12},{15,13},{18,16},{19,... | collective-permute-start | bytes 27656 | tf_op jit(solution)/shard_map/ppermute | solution.py:20
  12.3 2.6 %copy-start.7 = (s32[4]{0:T(128)S(1)}, s32[4]{0:T(128)}, u32[]{:S(2)}) copy-start(s32[4]{0:T(128)} %param.8) | copy-start | bytes 52
  12.3 3.6 %collective-permute-start.2 = (bf16[10,1,32]{1,2,0:T(8,128)(2,1)S(1)}, bf16[10,1,32]{1,2,0:T(8,128)(2,1)S(1)}, u32[]{:S(2)}, u32[]{:S(2)}) collective-permute-start(bf16[10,1,32]{1,2,0:T(8,128)(2,1)S(1)} %get-tuple-element.33), channel_id=1, source_target_pairs={{0,1},{2,3},{4,5},{6,7},{8,9},{10,11},{12,13},{14,15},{16,17},{18,... | collective-permute-start | bytes 1928 | tf_op jit(solution)/shard_map/ppermute | solution.py:18
  13.6 3.2 %collective-permute-start.3 = (bf16[10,1,32]{1,2,0:T(8,128)(2,1)S(1)}, bf16[10,1,32]{1,2,0:T(8,128)(2,1)S(1)}, u32[]{:S(2)}, u32[]{:S(2)}) collective-permute-start(bf16[10,1,32]{1,2,0:T(8,128)(2,1)S(1)} %get-tuple-element.34), channel_id=1, source_target_pairs={{1,0},{3,2},{5,4},{7,6},{9,8},{11,10},{13,12},{15,14},{17,16},{19,... | collective-permute-start | bytes 1928 | tf_op jit(solution)/shard_map/ppermute | solution.py:20
  17.9 0.7 %copy-start.3 = (bf16[288,32]{0,1:T(8,128)(2,1)S(1)}, bf16[288,32]{0,1:T(8,128)(2,1)}, u32[]{:S(2)}) copy-start(bf16[288,32]{0,1:T(8,128)(2,1)} %param.10) | copy-start | bytes 55300
  19.8 0.7 %copy-start.4 = (f32[32]{0:T(128)S(1)}, f32[32]{0:T(128)}, u32[]{:S(2)}) copy-start(f32[32]{0:T(128)} %param.11) | copy-start | bytes 388
  21.2 3.1 %collective-permute-start.4 = (bf16[1,72,32]{2,1,0:T(8,128)(2,1)S(1)}, bf16[1,72,32]{2,1,0:T(8,128)(2,1)S(1)}, u32[]{:S(2)}, u32[]{:S(2)}) collective-permute-start(bf16[1,72,32]{2,1,0:T(8,128)(2,1)S(1)} %get-tuple-element.45), channel_id=1, source_target_pairs={{0,2},{1,3},{4,6},{5,7},{8,10},{9,11},{12,14},{13,15},{16,18},{17,... | collective-permute-start | bytes 13832 | tf_op jit(solution)/shard_map/ppermute | solution.py:18
  22.9 5.7 %collective-permute-start.5 = (bf16[1,72,32]{2,1,0:T(8,128)(2,1)S(1)}, bf16[1,72,32]{2,1,0:T(8,128)(2,1)S(1)}, u32[]{:S(2)}, u32[]{:S(2)}) collective-permute-start(bf16[1,72,32]{2,1,0:T(8,128)(2,1)S(1)} %get-tuple-element.46), channel_id=1, source_target_pairs={{2,0},{3,1},{6,4},{7,5},{10,8},{11,9},{14,12},{15,13},{18,16},{19,... | collective-permute-start | bytes 13832 | tf_op jit(solution)/shard_map/ppermute | solution.py:20
  28.7 2.6 %collective-permute-start.6 = (bf16[6,1,32]{1,2,0:T(8,128)(2,1)S(1)}, bf16[6,1,32]{1,2,0:T(8,128)(2,1)S(1)}, u32[]{:S(2)}, u32[]{:S(2)}) collective-permute-start(bf16[6,1,32]{1,2,0:T(8,128)(2,1)S(1)} %get-tuple-element.50), channel_id=1, source_target_pairs={{0,1},{2,3},{4,5},{6,7},{8,9},{10,11},{12,13},{14,15},{16,17},{18,... | collective-permute-start | bytes 1160 | tf_op jit(solution)/shard_map/ppermute | solution.py:18
  30.0 3.1 %collective-permute-start.7 = (bf16[6,1,32]{1,2,0:T(8,128)(2,1)S(1)}, bf16[6,1,32]{1,2,0:T(8,128)(2,1)S(1)}, u32[]{:S(2)}, u32[]{:S(2)}) collective-permute-start(bf16[6,1,32]{1,2,0:T(8,128)(2,1)S(1)} %get-tuple-element.51), channel_id=1, source_target_pairs={{1,0},{3,2},{5,4},{7,6},{9,8},{11,10},{13,12},{15,14},{17,16},{19,... | collective-permute-start | bytes 1160 | tf_op jit(solution)/shard_map/ppermute | solution.py:20
  34.8 10.6 %all-to-all-start = ((bf16[4,3,2368]{2,1,0:T(4,128)(2,1)}), bf16[4,3,2368]{2,1,0:T(4,128)(2,1)S(1)}, u32[]{:S(2)}, u32[]{:S(2)}) async-start(bf16[4,3,2368]{2,1,0:T(4,128)(2,1)} %copy.96), calls=%async_computation | async-start | bytes 155648 | tf_op jit(solution)/shard_map/all_to_all | solution.py:52
  46.4 0.7 %copy-start = (bf16[4,3,74,32]{3,2,1,0:T(8,128)(2,1)}, bf16[4,3,74,32]{3,2,1,0:T(8,128)(2,1)S(1)}, u32[]{:S(2)}) copy-start(bf16[4,3,74,32]{3,2,1,0:T(8,128)(2,1)S(1)} %broadcast_select_fusion) | copy-start | bytes 170500
  47.2 0.8 %slice-start = ((bf16[4,3,74,32]{3,2,1,0:T(8,128)(2,1)}), bf16[1,3,74,32]{3,2,1,0:T(8,128)(2,1)S(1)}, s32[]{:S(2)}) async-start(bf16[4,3,74,32]{3,2,1,0:T(8,128)(2,1)} %copy-done), calls=%async_computation.1 | async-start | bytes 122880 | tf_op jit(solution)/shard_map/slice | solution.py:91
  48.6 0.9 %copy-start.2 = (bf16[864,64]{0,1:T(8,128)(2,1)S(1)}, bf16[864,64]{0,1:T(8,128)(2,1)}, u32[]{:S(2)}) copy-start(bf16[864,64]{0,1:T(8,128)(2,1)} %param.12) | copy-start | bytes 331780
  51.3 0.7 %copy-start.5 = (f32[64]{0:T(128)S(1)}, f32[64]{0:T(128)}, u32[]{:S(2)}) copy-start(f32[64]{0:T(128)} %param.13) | copy-start | bytes 772
where the time goes:
time: 53.9 us; the launch traced here: 53.4 us
  starting transfers between devices  19.1 us (35%)
  waiting for transfers between devices  16.7 us (31%)
  local copies, waits for them, and re-layouts  12.2 us (23%)
  matrix products  2.47 us (5%)
  other arithmetic  2.43 us (5%)
    ppermute x4, waiting for transfers between devices, extended(): lax.ppermute(head, axis, [((i + 1) % count, i) for i in range(ends)])  10.9 us
    ppermute x4, starting transfers between devices, extended(): lax.ppermute(tail, axis, [(i, (i + 1) % count) for i in range(ends)])  9.07 us
    all_to_all x1, waiting for transfers between devices, regroup(): lax.all_to_all(stacked, 'tm', split_axis=0, concat_axis=0, tiled=True)  5.77 us
    ppermute x4, starting transfers between devices, extended(): lax.ppermute(head, axis, [((i + 1) % count, i) for i in range(ends)])  5.17 us
    all_to_all x1, starting transfers between devices, regroup(): lax.all_to_all(stacked, 'tm', split_axis=0, concat_axis=0, tiled=True)  4.87 us
    unnamed x16, local copies, waits for them, and re-layouts  3.24 us
    dot_general x12, matrix products, conv_taps(): jnp.dot(patches, kernel, preferred_element_type=jnp.float32)  2.47 us
    slice x2, local copies, waits for them, and re-layouts, extended(): head = lax.slice_in_dim(cells, 0, width, axis=dim)  1.19 us
  transfers between devices with their start and end apart: 9, of which 5 were waited for; matrix products, arithmetic and copies ran while one was open for 3% of the time, Pallas kernels for 0%

commit v1 on v0

v1 whole, which is shorter than its diff:
```python
import functools

import jax
import jax.numpy as jnp
from jax import lax
from jax.experimental import pallas as pl
from jax.experimental.pallas import tpu as pltpu
from jax.sharding import PartitionSpec as P

CH = 32
OUTC = 64
LANES = 128
PX = LANES // CH
F32 = jnp.float32
BF16 = jnp.bfloat16
VMEM = pltpu.VMEM
SMEM = pltpu.SMEM


def up_to(value, step):
    return (value + step - 1) // step * step


def vm():
    return pl.BlockSpec(memory_space=pltpu.VMEM)


def sm():
    return pl.BlockSpec(memory_space=pltpu.SMEM)


def side(axis, toward):
    index = lax.axis_index(axis)
    if toward > 0:
        return index < lax.axis_size(axis) - 1
    return index > 0


def directions(axis):
    return (0,) if lax.axis_size(axis) <= 2 else (1, -1)


def halo_kernel(row_dirs, col_dirs, frames, valid, *refs):
    sends, marks = refs[:-1], refs[-1]
    height = frames.shape[1]
    lanes = frames.shape[2]
    blocks = valid.shape[2]
    last = valid.shape[1] - 1
    wide = lanes // blocks
    for block in range(blocks):
        window = pl.ds(block * wide, wide)
        for spot, line in ((0, last), (3, 0)):
            marks[spot : spot + 1, window] = jnp.full(
                (1, wide), valid[0, line, block].astype(F32), F32
            )
    spots = lax.broadcasted_iota(jnp.int32, (4, lanes), 0)
    tail = frames[0, height - 8 : height, :].astype(F32)[4:8]
    head = frames[0, 0:8, :].astype(F32)[0:4]
    down = jnp.where(spots == 0, marks[0:1, :], tail)
    upper = jnp.where(spots == 3, marks[3:4, :], head)
    bands = {1: down, -1: upper}
    bands[0] = jnp.where(side("row", 1), down, upper)
    columns = {}
    for way, first, block in ((1, lanes - LANES, blocks - 1), (-1, 0, 0)):
        edge = frames[0, :, first : first + LANES].astype(F32)
        flags = jnp.concatenate(
            [
                jnp.full((8, LANES), valid[0, line, block].astype(F32), F32)
                for line in range(last + 1)
            ],
            axis=0,
        )
        columns[way] = jnp.concatenate([edge, flags], axis=0)
    columns[0] = jnp.where(side("col", 1), columns[1], columns[-1])
    outs = iter(sends)
    for way in row_dirs:
        next(outs)[...] = bands[way].astype(BF16)
    for way in col_dirs:
        next(outs)[...] = columns[way].astype(BF16)
    for row_way in row_dirs:
        for col_way in col_dirs:
            right = bands[row_way][:, lanes - LANES :]
            left = bands[row_way][:, :LANES]
            if col_way == 0:
                picked = jnp.where(side("col", 1), right, left)
            else:
                picked = right if col_way > 0 else left
            next(outs)[...] = picked.astype(BF16)


def filter_matrix_kernel(weight, out):
    w = weight[...].astype(F32)
    tiled = jnp.concatenate([w] * PX, axis=1)
    taps = {
        (dy, dx): tiled[(3 * dy + dx) * CH : (3 * dy + dx + 1) * CH]
        for dy in range(3)
        for dx in range(3)
    }
    lane = lax.broadcasted_iota(jnp.int32, (CH, LANES), 1)
    line = lax.broadcasted_iota(jnp.int32, (CH, LANES), 0)
    nothing = jnp.zeros((CH, LANES), F32)
    for q in range(4):
        cell = []
        for v in range(4):
            terms = [
                taps[q - a, v - b]
                for a in range(2)
                for b in range(2)
                if 0 <= q - a < 3 and 0 <= v - b < 3
            ]
            cell.append(functools.reduce(jnp.add, terms) * 0.25)
        for u in range(-1, 2 * PX + 1):
            filt = nothing
            for p in range(PX):
                if 0 <= u - 2 * p + 1 < 4:
                    filt = jnp.where(lane // CH == p, cell[u - 2 * p + 1], filt)
            mean = nothing
            if 0 <= u < 2 * PX and q in (1, 2):
                mean = jnp.where(lane == u // 2 * CH + line, 0.25, nothing)
            spot = {-1: 2 * LANES + LANES - CH, 2 * PX: 2 * LANES}.get(u, u * CH)
            spot += q * 3 * LANES
            out[spot : spot + CH, :LANES] = filt.astype(BF16)
            out[spot : spot + CH, LANES:] = mean.astype(BF16)
        spot = q * 3 * LANES + 2 * LANES + CH
        out[spot : spot + LANES - 2 * CH, :] = jnp.zeros((LANES - 2 * CH, 2 * LANES), BF16)


def encoder_matrix_kernel(weight, out):
    w = weight[...].astype(F32)
    double = jnp.concatenate([w, w], axis=1)
    lane = lax.broadcasted_iota(jnp.int32, (CH, LANES), 1)
    nothing = jnp.zeros((CH, LANES), F32)
    wide = PX * OUTC
    for lag in range(3):
        for dy in range(3):
            base = (lag * 9 + dy * 3) * CH

            def tap(dx):
                if 0 <= dx < 3:
                    return double[base + dx * CH : base + (dx + 1) * CH]
                return nothing

            for u in range(-1, PX + 1):
                spot = {-1: 2 * LANES - CH, PX: LANES}.get(u, u * CH) + dy * 2 * LANES
                for half in range(PX // 2):
                    value = jnp.where(
                        lane < OUTC, tap(u - 2 * half + 1), tap(u - 2 * half)
                    )
                    first = lag * wide + half * LANES
                    out[spot : spot + CH, first : first + LANES] = value.astype(BF16)
            spot = dy * 2 * LANES + LANES + CH
            out[spot : spot + LANES - 2 * CH, lag * wide : (lag + 1) * wide] = jnp.zeros(
                (LANES - 2 * CH, wide), BF16
            )


def pool_kernel(
    order, stride, frames, valid, up, dn, rt, lf, ur, ul, dr, dl, matrix, bias, *refs
):
    outs, (x, pooled) = refs[:-2], refs[-2:]
    height = frames.shape[1]
    lanes = frames.shape[2]
    blocks = valid.shape[2]
    groups = lanes // LANES
    cells = groups // 2 + 1
    rows = height // 2
    held = pooled.shape[0] // outs[0].shape[1]
    has_up = side("row", -1).astype(F32)
    has_dn = side("row", 1).astype(F32)
    has_rt = side("col", 1).astype(F32)
    has_lf = side("col", -1).astype(F32)
    around = groups + 2
    pitch = x.shape[0] // around
    below = 8 + height
    blank = jnp.zeros((pitch - below, LANES), F32)
    right = rt[...].astype(F32) * has_rt
    left = lf[...].astype(F32) * has_lf
    for g in range(around):
        base = g * pitch
        window = pl.ds(g * LANES, LANES)
        if g < groups:
            own = frames[0, :, window].astype(F32)
            over = up[:, window].astype(F32) * has_up
            under = dn[:, window].astype(F32) * has_dn
        elif g == groups:
            own = right[:height]
            over = ur[...].astype(F32) * (has_up * has_rt)
            under = dr[...].astype(F32) * (has_dn * has_rt)
        else:
            own = left[:height]
            over = ul[...].astype(F32) * (has_up * has_lf)
            under = dl[...].astype(F32) * (has_dn * has_lf)
        x[base : base + 4, :] = jnp.zeros((4, LANES), F32)
        x[base + 4 : base + 8, :] = over
        x[base + 8 : base + below, :] = own
        x[base + below : base + pitch, :] = blank
        x[base + below : base + below + 4, :] = under

    lane = lax.broadcasted_iota(jnp.int32, (held, LANES), 1)
    spot = lax.broadcasted_iota(jnp.int32, (held, LANES), 0)
    pieces = []
    for q in range(4):
        strips = [
            x[pl.ds(g * pitch + 5 + q, held, stride=2), :] for g in range(around)
        ]
        pieces.append(jnp.concatenate([strips[2 * c] for c in range(cells)], axis=0))
        pieces.append(jnp.concatenate([strips[2 * c + 1] for c in range(cells)], axis=0))
        pieces.append(
            jnp.concatenate(
                [
                    jnp.where(
                        lane < LANES // 2,
                        strips[(2 * c + 2) % around],
                        strips[(2 * c - 1) % around],
                    )
                    for c in range(cells)
                ],
                axis=0,
            )
        )
    patches = jnp.concatenate([piece.astype(BF16) for piece in pieces], axis=1)
    result = jnp.dot(patches, matrix[...], preferred_element_type=F32)
    shift = jnp.concatenate([bias[...]] * PX, axis=1)
    for c in range(cells):
        if c < blocks:
            base = 2 * c * pitch
            above = x[base + 4 : base + 5, :]
            under = x[base + below + 3 : base + below + 4, :]
            inside = [valid[0, line, c].astype(F32) for line in range(valid.shape[1])]
        else:
            one = lax.broadcasted_iota(jnp.int32, (1, LANES), 1) < LANES // 2

            def both(line):
                first = groups * pitch + line
                second = first + pitch
                return jnp.where(one, x[first : first + 1, :], x[second : second + 1, :])

            above, under = both(4), both(below + 3)
            inside = [
                jnp.where(
                    one,
                    right[height + 8 * line : height + 8 * line + 1],
                    left[height + 8 * line : height + 8 * line + 1],
                )
                for line in range(valid.shape[1])
            ]
        mask = jnp.where(spot == 0, above, jnp.zeros((held, LANES), F32))
        mask = jnp.where(spot == rows + 1, under, mask)
        for line, value in enumerate(inside):
            mask = jnp.where((spot >= 1 + 4 * line) & (spot < 5 + 4 * line), value, mask)
        part = result[c * held : (c + 1) * held]
        pooled[c * held : (c + 1) * held, :] = part[:, LANES:] + mask * (part[:, :LANES] + shift)
    me = lax.axis_index("tm")
    for out, step in zip(outs, order):
        band = step(me)
        for dy in range(stride + 2):
            out[dy] = pooled[pl.ds(band * stride + dy, out.shape[1], stride=held), :].astype(BF16)


def encode_kernel(sources, owner, matrix, bias, *refs):
    count = len(sources)
    arrived = refs[:count]
    out, chunks, folded = refs[count:]
    frames = chunks.shape[0]
    me = lax.axis_index("tm")
    for piece, source in zip(arrived, sources):
        if source is None:
            for slot in range(frames):
                chunks[owner[slot]] = piece[slot].astype(F32)
        else:
            chunks[owner[source(me)]] = piece[...].astype(F32)
    cells = out.shape[3] // (PX * OUTC)
    stride = out.shape[1]
    held = chunks.shape[2]
    kept = up_to(cells, 8)
    lane = lax.broadcasted_iota(jnp.int32, (kept, LANES), 1)
    wide = PX * OUTC
    shift = jnp.concatenate([bias[...]] * PX, axis=1)
    pitch = folded.shape[1] // kept
    for line in range(stride):
        lines = []
        for dy in range(3):
            now, beside = [], []
            for t in range(frames):
                full = chunks[t, line + dy]
                ahead = pltpu.roll(full, held - 1, 0)
                behind = pltpu.roll(full, 1, 0)
                first = lax.broadcasted_iota(jnp.int32, (held, LANES), 0) == 0
                behind = jnp.where(first, full[cells : cells + 1], behind)
                now.append(full[:kept])
                beside.append(jnp.where(lane < LANES // 2, ahead[:kept], behind[:kept]))
            lines.append(jnp.concatenate(now, axis=0).astype(BF16))
            lines.append(jnp.concatenate(beside, axis=0).astype(BF16))
        patches = jnp.concatenate(lines, axis=1)
        result = jnp.dot(patches, matrix[...], preferred_element_type=F32)
        for j in range(frames - 1):
            total = shift
            for lag in range(3):
                t = max(j + 1 - lag, 0)
                total = total + result[t * kept : (t + 1) * kept, lag * wide : (lag + 1) * wide]
            for half in range(wide // LANES):
                folded[half, pl.ds(j, kept, stride=pitch), :] = total[
                    :, half * LANES : (half + 1) * LANES
                ]
        for g in range(cells):
            for half in range(wide // LANES):
                first = g * wide + half * LANES
                out[0, line, :, first : first + LANES] = folded[
                    half, g * pitch : g * pitch + frames - 1, :
                ].astype(BF16)


def ring(axis, shift):
    count = lax.axis_size(axis)
    return [(i, i + shift) for i in range(count) if 0 <= i + shift < count]


def pairs_of(axis, way):
    count = lax.axis_size(axis)
    if way == 0:
        return [(i, count - 1 - i) for i in range(count)]
    return ring(axis, way)


def call(kernel, outs, specs, scratch, name, work=(0, 0)):
    return pl.pallas_call(
        kernel,
        out_shape=outs,
        in_specs=specs,
        out_specs=jax.tree.map(lambda _: vm(), outs),
        scratch_shapes=scratch,
        name=name,
        cost_estimate=pl.CostEstimate(flops=work[0], bytes_accessed=work[1], transcendentals=0),
    )


def on_device(
    frames, owner_map, valid_blocks, deblock_weight, deblock_bias, encoder_weight, encoder_bias
):
    height = frames.shape[1]
    lanes = frames.shape[2]
    bands = lax.axis_size("tm")
    shaped = jax.ShapeDtypeStruct
    row_dirs, col_dirs = directions("row"), directions("col")
    n_col = lax.axis_size("col")

    band = shaped((4, lanes), BF16)
    column = shaped((2 * height, LANES), BF16)
    corner = shaped((4, LANES), BF16)
    sends = call(
        functools.partial(halo_kernel, row_dirs, col_dirs),
        [band] * len(row_dirs)
        + [column] * len(col_dirs)
        + [corner] * (len(row_dirs) * len(col_dirs)),
        [vm(), sm()],
        [VMEM((8, lanes), F32)],
        "halo",
    )(frames, valid_blocks)
    sends = iter(sends)
    by_row = {w: lax.ppermute(next(sends), "row", pairs_of("row", w)) for w in row_dirs}
    by_col = {w: lax.ppermute(next(sends), "col", pairs_of("col", w)) for w in col_dirs}
    by_both = {}
    for w in row_dirs:
        for v in col_dirs:
            pairs = [
                (a * n_col + c, b * n_col + d)
                for a, b in pairs_of("row", w)
                for c, d in pairs_of("col", v)
            ]
            by_both[w, v] = lax.ppermute(next(sends), ("row", "col"), pairs)

    def pick(table, way):
        return table[way] if way in table else table[0]

    def pick_both(w, v):
        return by_both[w if w in row_dirs else 0, v if v in col_dirs else 0]

    filter_matrix = call(
        filter_matrix_kernel,
        shaped((12 * LANES, 2 * LANES), BF16),
        [vm()],
        [],
        "filter_matrix",
        (1 << 22, 1 << 20),
    )(deblock_weight)
    encoder_matrix = call(
        encoder_matrix_kernel,
        shaped((6 * LANES, 3 * PX * OUTC), BF16),
        [vm()],
        [],
        "encoder_matrix",
        (1 << 22, 1 << 20),
    )(encoder_weight)

    rows = height // 2
    stride = rows // bands
    cells = lanes // LANES // 2 + 1
    held = up_to(rows + 2, 8)
    kept = up_to(cells, 8)
    piece = shaped((stride + 2, kept, LANES), BF16)
    direct = bands <= 4 and bands & (bands - 1) == 0
    if direct:
        order = [functools.partial(lambda k, me: me ^ k, k) for k in range(bands)]
    else:
        order = [functools.partial(lambda k, me: k, k) for k in range(bands)]
    parts = call(
        functools.partial(pool_kernel, order, stride),
        [piece] * bands,
        [vm(), sm()] + [vm()] * 10,
        [
            VMEM(((lanes // LANES + 2) * up_to(8 + 2 * held, 8), LANES), F32),
            VMEM((kept * held, LANES), F32),
        ],
        "pool",
        (1 << 22, 1 << 20),
    )(
        frames,
        valid_blocks,
        pick(by_row, 1),
        pick(by_row, -1),
        pick(by_col, -1),
        pick(by_col, 1),
        pick_both(1, -1),
        pick_both(1, 1),
        pick_both(-1, -1),
        pick_both(-1, 1),
        filter_matrix,
        deblock_bias.reshape(1, CH),
    )
    if direct:
        arrived = [parts[0]] + [
            lax.ppermute(parts[k], "tm", [(i, i ^ k) for i in range(bands)])
            for k in range(bands - 1, 0, -1)
        ]
        sources = [order[0]] + [order[k] for k in range(bands - 1, 0, -1)]
    else:
        arrived = [
            lax.all_to_all(jnp.stack(parts), "tm", split_axis=0, concat_axis=0, tiled=True)
        ]
        sources = [None]
    encoded = call(
        functools.partial(encode_kernel, sources),
        shaped((1, stride, bands - 1, lanes // 2 // CH * OUTC), BF16),
        [sm(), vm(), vm()] + [vm()] * len(arrived),
        [
            VMEM((bands, stride + 2, kept, LANES), F32),
            VMEM((PX * OUTC // LANES, kept * up_to(bands - 1, 8), LANES), F32),
        ],
        "encode",
        (1 << 22, 1 << 20),
    )(owner_map, encoder_matrix, encoder_bias.reshape(1, OUTC), *arrived)
    return encoded.transpose(2, 0, 1, 3)


def solution(mesh):
    return jax.shard_map(
        on_device,
        mesh=mesh,
        in_specs=(
            P(("grp", "tm"), "row", "col"),
            P("grp"),
            P(("grp", "tm"), "row", "col"),
            P(),
            P(),
            P(),
            P(),
        ),
        out_specs=P("grp", "row", "tm", "col"),
        check_vma=False,
    )
```

time: 53.9 us -> 23.2 us (0.43)
  waiting for transfers between devices: 16.7 us -> 1.2 us
  starting transfers between devices: 19.1 us -> 7.85 us
  Pallas kernels: 0 us -> 10.3 us
  local copies, waits for them, and re-layouts: 12.2 us -> 3.53 us
  matrix products: 2.47 us -> 0 us
  other arithmetic: 2.43 us -> 0 us
    pallas_call x0 -> x5, Pallas kernels: none -> 10.3 us  [the longest x1 2.29 us: on_device(): call(functools.partial(encode_kernel, sources), shaped((1, stride, bands...]
    ppermute x8 -> x6, waiting for transfers between devices: 10.9 us -> 1.2 us  [the longest x3 1.19 us: on_device(): lax.ppermute(parts[k], 'tm', [(i, i ^ k) for i in range(bands)])]
    ppermute x8 -> x6, starting transfers between devices: 14.2 us -> 7.85 us  [the longest x3 4.77 us: on_device(): lax.ppermute(parts[k], 'tm', [(i, i ^ k) for i in range(bands)])]
    all_to_all x1 -> x0, waiting for transfers between devices: 5.77 us -> none  [regroup(): lax.all_to_all(stacked, 'tm', split_axis=0, concat_axis=0, tiled=True)]
    all_to_all x1 -> x0, starting transfers between devices: 4.87 us -> none  [regroup(): lax.all_to_all(stacked, 'tm', split_axis=0, concat_axis=0, tiled=True)]
    slice x19 -> x0, local copies, waits for them, and re-layouts: 3.58 us -> none  [the longest x2 1.19 us: extended(): head = lax.slice_in_dim(cells, 0, width, axis=dim)]
    dot_general x12 -> x0, matrix products: 2.47 us -> none  [conv_taps(): jnp.dot(patches, kernel, preferred_element_type=jnp.float32)]
    concatenate x10 -> x0, local copies, waits for them, and re-layouts: 2 us -> none  [the longest x4 1.05 us: on_device(): stacked = jnp.concatenate([upper, middle, lower], axis=1)]
  transfers between devices with their start and end apart: 9 -> 6, of which waited for: 5 -> 1; matrix products, arithmetic and copies ran while one was open for 3% -> 10% of each run, Pallas kernels for 0% -> 18%
where the time goes in v1:
time: 23.2 us; the launch traced here: 22.9 us
  Pallas kernels  10.3 us (44%)
  starting transfers between devices  7.85 us (34%)
  local copies, waits for them, and re-layouts  3.53 us (15%)
  waiting for transfers between devices  1.2 us (5%)
    ppermute x3, starting transfers between devices, on_device(): lax.ppermute(parts[k], 'tm', [(i, i ^ k) for i in range(bands)])  4.77 us
    unnamed x16, local copies, waits for them, and re-layouts  3.53 us
    ppermute x1, starting transfers between devices, on_device(): lax.ppermute(next(sends), 'row', pairs_of('row', w))  2.97 us
    pallas_call x1, Pallas kernels, on_device(): call(functools.partial(encode_kernel, sources), shaped((1, stride, bands...  2.29 us
    pallas_call x1, Pallas kernels, on_device(): call(encoder_matrix_kernel, shaped((6 * LANES, 3 * PX * OUTC), BF16), [vm...  2.19 us
    pallas_call x1, Pallas kernels, on_device(): call(functools.partial(pool_kernel, order, stride), [piece] * bands, [vm(...  2.17 us
    pallas_call x1, Pallas kernels, on_device(): call(filter_matrix_kernel, shaped((12 * LANES, 2 * LANES), BF16), [vm()],...  2.03 us
    pallas_call x1, Pallas kernels, on_device(): call(functools.partial(halo_kernel, row_dirs, col_dirs), [band] * len(row...  1.61 us
  transfers between devices with their start and end apart: 6, of which 1 were waited for; matrix products, arithmetic and copies ran while one was open for 10% of the time, Pallas kernels for 18%

profile of v1, /device:TPU:0, one launch (start us, length us, event | category | flops | bytes accessed | tf_op | source)
XLA Modules:
  0.0 22.9 jit_solution(18203759657315342273)
XLA Ops:
  0.0 1.6 %halo.1 = (bf16[4,4608]{1,0:T(4,128)(2,1)}, bf16[16,128]{1,0:T(8,128)(2,1)}, bf16[4,128]{1,0:T(4,128)(2,1)}) custom-call(bf16[1,8,4608]{2,1,0:T(8,128)(2,1)} %frames.3, s32[1,1,18]{2,1,0:T(1,128)} %valid.3), custom_call_target="tpu_custom_call" | custom-call | tf_op jit(solution)/shard_map/halo/pallas_call | solution.py:350
  1.6 3.0 %collective-permute-start = (bf16[4,4608]{1,0:T(4,128)(2,1)}, bf16[4,4608]{1,0:T(4,128)(2,1)S(1)}, u32[]{:S(2)}, u32[]{:S(2)}) collective-permute-start(bf16[4,4608]{1,0:T(4,128)(2,1)} %get-tuple-element.12), channel_id=1, source_target_pairs={{0,2},{2,0},{1,3},{3,1},{4,6},{6,4},{5,7},{7,5},{8,10},{10,8},{9,1... | collective-permute-start | bytes 110600 | tf_op jit(solution)/shard_map/ppermute | solution.py:360
  4.6 0.0 collective-permute-start.1
  4.6 0.1 collective-permute-start.2
  4.7 1.5 %copy.9.weight = bf16[288,32]{1,0:T(8,128)(2,1)} copy(bf16[288,32]{0,1:T(8,128)(2,1)} %param.10) | data formatting | bytes 36864 | tf_op args[3]
  6.2 2.0 %filter_matrix.1.matrix = bf16[1536,256]{1,0:T(8,128)(2,1)} custom-call(bf16[288,32]{1,0:T(8,128)(2,1)} %copy.9.weight), custom_call_target="tpu_custom_call" | custom-call | flops 4194304 | bytes 1048576 | tf_op jit(solution)/shard_map/filter_matrix/pallas_call | solution.py:378
  8.2 0.0 collective-permute-done.2.ur.ul.dr.dl
  8.2 0.0 collective-permute-done.1.rt.lf
  8.2 0.0 copy-start
  8.2 0.5 %copy-done.6 = bf16[4,128]{1,0:T(4,128)(2,1)} copy-done((bf16[4,128]{1,0:T(4,128)(2,1)}, bf16[4,128]{1,0:T(4,128)(2,1)S(1)}, u32[]{:S(2)}) %copy-start.6) | copy-done | bytes 1048
  8.8 0.0 copy-done.5
  8.8 0.0 copy-done
  8.8 2.2 %pool.1 = (bf16[3,24,128]{2,1,0:T(8,128)(2,1)}, bf16[3,24,128]{2,1,0:T(8,128)(2,1)}, bf16[3,24,128]{2,1,0:T(8,128)(2,1)}, bf16[3,24,128]{2,1,0:T(8,128)(2,1)}) custom-call(bf16[1,8,4608]{2,1,0:T(8,128)(2,1)} %frames.3, s32[1,1,18]{2,1,0:T(1,128)} %valid.3, bf16[4,4608]{1,0:T(4,128)(2,1)} %copy-done, bf16[4,4608]{1,0:T(4,128)(2,1)} %copy-done, ...), custom_call_target="tpu_custom_call" | custom-call | flops 4194304 | bytes 1048576 | tf_op jit(solution)/shard_map/pool/pallas_call | solution.py:406
  11.0 4.1 %collective-permute-start.3 = (bf16[3,24,128]{2,1,0:T(8,128)(2,1)}, bf16[3,24,128]{2,1,0:T(8,128)(2,1)S(1)}, u32[]{:S(2)}, u32[]{:S(2)}) collective-permute-start(bf16[3,24,128]{2,1,0:T(8,128)(2,1)} %get-tuple-element.16), channel_id=1, source_target_pairs={{0,12},{4,8},{8,4},{12,0},{1,13},{5,9},{9,5},{13,1},{2,14},{6,10},... | collective-permute-start | bytes 55304 | tf_op jit(solution)/shard_map/ppermute | solution.py:432
  15.2 0.0 collective-permute-start.4
  15.2 0.6 %collective-permute-start.5 = (bf16[3,24,128]{2,1,0:T(8,128)(2,1)}, bf16[3,24,128]{2,1,0:T(8,128)(2,1)S(1)}, u32[]{:S(2)}, u32[]{:S(2)}) collective-permute-start(bf16[3,24,128]{2,1,0:T(8,128)(2,1)} %get-tuple-element.18), channel_id=1, source_target_pairs={{0,4},{4,0},{8,12},{12,8},{1,5},{5,1},{9,13},{13,9},{2,6},{6,2},{1... | collective-permute-start | bytes 55304 | tf_op jit(solution)/shard_map/ppermute | solution.py:432
  15.8 0.8 %copy.8.weight = bf16[864,64]{1,0:T(8,128)(2,1)} copy(bf16[864,64]{0,1:T(8,128)(2,1)S(1)} %copy-done.1) | data formatting | bytes 221184 | tf_op args[5]
  16.6 2.2 %encoder_matrix.1.matrix = bf16[768,768]{1,0:T(8,128)(2,1)} custom-call(bf16[864,64]{1,0:T(8,128)(2,1)} %copy.8.weight), custom_call_target="tpu_custom_call" | custom-call | flops 4194304 | bytes 1048576 | tf_op jit(solution)/shard_map/encoder_matrix/pallas_call | solution.py:386
  18.8 0.0 collective-permute-done.3.refs_1_
  18.8 1.2 %collective-permute-done.4.refs_2_ = bf16[3,24,128]{2,1,0:T(8,128)(2,1)S(1)} collective-permute-done((bf16[3,24,128]{2,1,0:T(8,128)(2,1)}, bf16[3,24,128]{2,1,0:T(8,128)(2,1)S(1)}, u32[]{:S(2)}, u32[]{:S(2)}) %collective-permute-start.4) | collective-permute-done | bytes 18464 | tf_op jit(solution)/shard_map/ppermute | solution.py:432
  20.0 0.0 collective-permute-done.5.refs_3_
  20.0 0.6 %copy-done.3 = bf16[3,24,128]{2,1,0:T(8,128)(2,1)} copy-done((bf16[3,24,128]{2,1,0:T(8,128)(2,1)}, bf16[3,24,128]{2,1,0:T(8,128)(2,1)S(1)}, u32[]{:S(2)}) %copy-start.3) | copy-done | bytes 18456
  20.6 0.0 copy-done.4
  20.6 2.3 %encode.1 = bf16[1,1,3,4608]{3,2,1,0:T(4,128)(2,1)} custom-call(s32[4]{0:T(128)} %owner.1, bf16[768,768]{1,0:T(8,128)(2,1)} %encoder_matrix.1.matrix, f32[1,64]{1,0:T(1,128)} %bitcast.4, bf16[3,24,128]{2,1,0:T(8,128)(2,1)} %get-tuple-element.15.refs_0_, bf16[3,24,128]{2,1,0:T(8,128)(2,1)} %copy-done.2, bf16[3,24,128]{2,1,0:T(8,128)(2,1)} %copy-done.3, ...), custom_call_target="tpu_custom_call" | custom-call | flops 4194304 | bytes 1048576 | tf_op jit(solution)/shard_map/encode/pallas_call | solution.py:441
  (9 shorter events, 0.0 us)
Async XLA Ops:
  0.0 15.8 %copy-start.1 = (bf16[864,64]{0,1:T(8,128)(2,1)S(1)}, bf16[864,64]{0,1:T(8,128)(2,1)}, u32[]{:S(2)}) copy-start(bf16[864,64]{0,1:T(8,128)(2,1)} %param.12) | copy-start | bytes 331780
  1.6 6.6 %collective-permute-start = (bf16[4,4608]{1,0:T(4,128)(2,1)}, bf16[4,4608]{1,0:T(4,128)(2,1)S(1)}, u32[]{:S(2)}, u32[]{:S(2)}) collective-permute-start(bf16[4,4608]{1,0:T(4,128)(2,1)} %get-tuple-element.12), channel_id=1, source_target_pairs={{0,2},{2,0},{1,3},{3,1},{4,6},{6,4},{5,7},{7,5},{8,10},{10,8},{9,1... | collective-permute-start | bytes 110600 | tf_op jit(solution)/shard_map/ppermute | solution.py:360
  4.6 3.6 %collective-permute-start.1 = (bf16[16,128]{1,0:T(8,128)(2,1)}, bf16[16,128]{1,0:T(8,128)(2,1)S(1)}, u32[]{:S(2)}, u32[]{:S(2)}) collective-permute-start(bf16[16,128]{1,0:T(8,128)(2,1)} %get-tuple-element.13), channel_id=1, source_target_pairs={{0,1},{1,0},{2,3},{3,2},{4,5},{5,4},{6,7},{7,6},{8,9},{9,8},{10,11... | collective-permute-start | bytes 12296 | tf_op jit(solution)/shard_map/ppermute | solution.py:361
  4.6 3.6 %collective-permute-start.2 = (bf16[4,128]{1,0:T(4,128)(2,1)}, bf16[4,128]{1,0:T(4,128)(2,1)S(1)}, u32[]{:S(2)}, u32[]{:S(2)}) collective-permute-start(bf16[4,128]{1,0:T(4,128)(2,1)} %get-tuple-element.14), channel_id=1, source_target_pairs={{0,3},{1,2},{2,1},{3,0},{4,7},{5,6},{6,5},{7,4},{8,11},{9,10},{10,... | collective-permute-start | bytes 3080 | tf_op jit(solution)/shard_map/ppermute | solution.py:370
  8.2 0.6 %copy-start.6 = (bf16[4,128]{1,0:T(4,128)(2,1)}, bf16[4,128]{1,0:T(4,128)(2,1)S(1)}, u32[]{:S(2)}) copy-start(bf16[4,128]{1,0:T(4,128)(2,1)S(1)} %collective-permute-done.2.ur.ul.dr.dl) | copy-start | bytes 3076
  8.2 0.6 %copy-start.5 = (bf16[16,128]{1,0:T(8,128)(2,1)}, bf16[16,128]{1,0:T(8,128)(2,1)S(1)}, u32[]{:S(2)}) copy-start(bf16[16,128]{1,0:T(8,128)(2,1)S(1)} %collective-permute-done.1.rt.lf) | copy-start | bytes 12292
  8.2 0.6 %copy-start = (bf16[4,4608]{1,0:T(4,128)(2,1)}, bf16[4,4608]{1,0:T(4,128)(2,1)S(1)}, u32[]{:S(2)}) copy-start(bf16[4,4608]{1,0:T(4,128)(2,1)S(1)} %collective-permute-done.up.dn) | copy-start | bytes 110596
  11.0 7.8 %collective-permute-start.3 = (bf16[3,24,128]{2,1,0:T(8,128)(2,1)}, bf16[3,24,128]{2,1,0:T(8,128)(2,1)S(1)}, u32[]{:S(2)}, u32[]{:S(2)}) collective-permute-start(bf16[3,24,128]{2,1,0:T(8,128)(2,1)} %get-tuple-element.16), channel_id=1, source_target_pairs={{0,12},{4,8},{8,4},{12,0},{1,13},{5,9},{9,5},{13,1},{2,14},{6,10},... | collective-permute-start | bytes 55304 | tf_op jit(solution)/shard_map/ppermute | solution.py:432
  15.2 4.9 %collective-permute-start.4 = (bf16[3,24,128]{2,1,0:T(8,128)(2,1)}, bf16[3,24,128]{2,1,0:T(8,128)(2,1)S(1)}, u32[]{:S(2)}, u32[]{:S(2)}) collective-permute-start(bf16[3,24,128]{2,1,0:T(8,128)(2,1)} %get-tuple-element.17), channel_id=1, source_target_pairs={{0,8},{4,12},{8,0},{12,4},{1,9},{5,13},{9,1},{13,5},{2,10},{6,14},... | collective-permute-start | bytes 55304 | tf_op jit(solution)/shard_map/ppermute | solution.py:432
  15.2 4.9 %collective-permute-start.5 = (bf16[3,24,128]{2,1,0:T(8,128)(2,1)}, bf16[3,24,128]{2,1,0:T(8,128)(2,1)S(1)}, u32[]{:S(2)}, u32[]{:S(2)}) collective-permute-start(bf16[3,24,128]{2,1,0:T(8,128)(2,1)} %get-tuple-element.18), channel_id=1, source_target_pairs={{0,4},{4,0},{8,12},{12,8},{1,5},{5,1},{9,13},{13,9},{2,6},{6,2},{1... | collective-permute-start | bytes 55304 | tf_op jit(solution)/shard_map/ppermute | solution.py:432
  18.8 1.2 %copy-start.2 = (bf16[3,24,128]{2,1,0:T(8,128)(2,1)}, bf16[3,24,128]{2,1,0:T(8,128)(2,1)S(1)}, u32[]{:S(2)}) copy-start(bf16[3,24,128]{2,1,0:T(8,128)(2,1)S(1)} %collective-permute-done.3.refs_1_) | copy-start | bytes 55300
  20.0 0.6 %copy-start.3 = (bf16[3,24,128]{2,1,0:T(8,128)(2,1)}, bf16[3,24,128]{2,1,0:T(8,128)(2,1)S(1)}, u32[]{:S(2)}) copy-start(bf16[3,24,128]{2,1,0:T(8,128)(2,1)S(1)} %collective-permute-done.4.refs_2_) | copy-start | bytes 55300
  20.0 0.6 %copy-start.4 = (bf16[3,24,128]{2,1,0:T(8,128)(2,1)}, bf16[3,24,128]{2,1,0:T(8,128)(2,1)S(1)}, u32[]{:S(2)}) copy-start(bf16[3,24,128]{2,1,0:T(8,128)(2,1)S(1)} %collective-permute-done.5.refs_3_) | copy-start | bytes 55300

commit v2 on v1

--- a/solution.py
+++ b/solution.py
@@ -15,6 +15,7 @@
 BF16 = jnp.bfloat16
 VMEM = pltpu.VMEM
 SMEM = pltpu.SMEM
+DMA = pltpu.SemaphoreType.DMA
 
 
 def up_to(value, step):
@@ -25,8 +26,23 @@
     return pl.BlockSpec(memory_space=pltpu.VMEM)
 
 
-def sm():
-    return pl.BlockSpec(memory_space=pltpu.SMEM)
+def far():
+    return pl.BlockSpec(memory_space=pltpu.HBM)
+
+
+def in_far(array):
+    return pltpu.with_memory_space_constraint(array, pltpu.HBM)
+
+
+def fetch(*pairs):
+    *pairs, sems = pairs
+    copies = [
+        pltpu.make_async_copy(source, target, sems.at[i])
+        for i, (source, target) in enumerate(pairs)
+    ]
+    for copy in copies:
+        copy.start()
+    return copies
 
 
 def side(axis, toward):
@@ -40,8 +56,10 @@
     return (0,) if lax.axis_size(axis) <= 2 else (1, -1)
 
 
-def halo_kernel(row_dirs, col_dirs, frames, valid, *refs):
-    sends, marks = refs[:-1], refs[-1]
+def halo_kernel(row_dirs, col_dirs, frames_far, valid_far, frames, *refs):
+    sends, (marks, valid, sems) = refs[:-3], refs[-3:]
+    whole, flags = fetch((frames_far, frames), (valid_far, valid), sems)
+    flags.wait()
     height = frames.shape[1]
     lanes = frames.shape[2]
     blocks = valid.shape[2]
@@ -53,6 +71,7 @@
             marks[spot : spot + 1, window] = jnp.full(
                 (1, wide), valid[0, line, block].astype(F32), F32
             )
+    whole.wait()
     spots = lax.broadcasted_iota(jnp.int32, (4, lanes), 0)
     tail = frames[0, height - 8 : height, :].astype(F32)[4:8]
     head = frames[0, 0:8, :].astype(F32)[0:4]
@@ -88,9 +107,34 @@
             next(outs)[...] = picked.astype(BF16)
 
 
-def filter_matrix_kernel(weight, out):
-    w = weight[...].astype(F32)
-    tiled = jnp.concatenate([w] * PX, axis=1)
+def turned(weight, staged):
+    count = LANES // weight.shape[0]
+    values = weight[...].astype(F32)
+    staged[:, : values.shape[1]] = jnp.concatenate([values] * count, axis=0)
+    return jnp.concatenate(
+        [
+            jnp.transpose(staged[:, first : first + LANES])
+            for first in range(0, staged.shape[1], LANES)
+        ],
+        axis=0,
+    )
+
+
+def filter_matrix_kernel(
+    held, weight_far, bias_far, valid_far, out, shift, masks, weight, bias, valid, staged, sems
+):
+    copies = fetch((weight_far, weight), (bias_far, bias), (valid_far, valid), sems)
+    for copy in copies:
+        copy.wait()
+    shift[...] = jnp.broadcast_to(jnp.concatenate([bias[...]] * PX, axis=1), shift.shape)
+    spots = lax.broadcasted_iota(jnp.int32, (held, LANES), 0)
+    for c in range(valid.shape[2]):
+        mask = jnp.zeros((held, LANES), F32)
+        for line in range(valid.shape[1]):
+            inside = (spots >= 1 + 4 * line) & (spots < 5 + 4 * line)
+            mask = jnp.where(inside, valid[0, line, c].astype(F32), mask)
+        masks[c * held : (c + 1) * held, :] = mask
+    tiled = turned(weight, staged)
     taps = {
         (dy, dx): tiled[(3 * dy + dx) * CH : (3 * dy + dx + 1) * CH]
         for dy in range(3)
@@ -125,9 +169,18 @@
         out[spot : spot + LANES - 2 * CH, :] = jnp.zeros((LANES - 2 * CH, 2 * LANES), BF16)
 
 
-def encoder_matrix_kernel(weight, out):
-    w = weight[...].astype(F32)
-    double = jnp.concatenate([w, w], axis=1)
+def encoder_matrix_kernel(
+    sources, weight_far, bias_far, owner_far, out, shift, picks, weight, bias, owner, staged, sems
+):
+    copies = fetch((weight_far, weight), (bias_far, bias), (owner_far, owner), sems)
+    for copy in copies:
+        copy.wait()
+    shift[...] = jnp.broadcast_to(jnp.concatenate([bias[...]] * PX, axis=1), shift.shape)
+    me = lax.axis_index("tm")
+    for spot, source in enumerate(sources):
+        time = jnp.full(picks.shape[1:], owner[source(me)], jnp.int32)
+        picks[spot] = time
+    double = turned(weight, staged)
     lane = lax.broadcasted_iota(jnp.int32, (CH, LANES), 1)
     nothing = jnp.zeros((CH, LANES), F32)
     wide = PX * OUTC
@@ -155,13 +208,13 @@
 
 
 def pool_kernel(
-    order, stride, frames, valid, up, dn, rt, lf, ur, ul, dr, dl, matrix, bias, *refs
+    order, stride, frames, up, dn, rt, lf, ur, ul, dr, dl, matrix, bias, masks, *refs
 ):
     outs, (x, pooled) = refs[:-2], refs[-2:]
     height = frames.shape[1]
     lanes = frames.shape[2]
-    blocks = valid.shape[2]
     groups = lanes // LANES
+    blocks = groups // 2
     cells = groups // 2 + 1
     rows = height // 2
     held = pooled.shape[0] // outs[0].shape[1]
@@ -220,13 +273,15 @@
         )
     patches = jnp.concatenate([piece.astype(BF16) for piece in pieces], axis=1)
     result = jnp.dot(patches, matrix[...], preferred_element_type=F32)
-    shift = jnp.concatenate([bias[...]] * PX, axis=1)
+    shift = bias[0:1, :]
     for c in range(cells):
+        mask = jnp.zeros((held, LANES), F32)
         if c < blocks:
             base = 2 * c * pitch
             above = x[base + 4 : base + 5, :]
             under = x[base + below + 3 : base + below + 4, :]
-            inside = [valid[0, line, c].astype(F32) for line in range(valid.shape[1])]
+            mask = masks[c * held : (c + 1) * held, :]
+            inside = []
         else:
             one = lax.broadcasted_iota(jnp.int32, (1, LANES), 1) < LANES // 2
 
@@ -242,9 +297,9 @@
                     right[height + 8 * line : height + 8 * line + 1],
                     left[height + 8 * line : height + 8 * line + 1],
                 )
-                for line in range(valid.shape[1])
+                for line in range(height // 8)
             ]
-        mask = jnp.where(spot == 0, above, jnp.zeros((held, LANES), F32))
+        mask = jnp.where(spot == 0, above, mask)
         mask = jnp.where(spot == rows + 1, under, mask)
         for line, value in enumerate(inside):
             mask = jnp.where((spot >= 1 + 4 * line) & (spot < 5 + 4 * line), value, mask)
@@ -257,25 +312,27 @@
             out[dy] = pooled[pl.ds(band * stride + dy, out.shape[1], stride=held), :].astype(BF16)
 
 
-def encode_kernel(sources, owner, matrix, bias, *refs):
-    count = len(sources)
-    arrived = refs[:count]
-    out, chunks, folded = refs[count:]
+def encode_kernel(matrix, bias, picks, *refs):
+    arrived, (out, chunks, folded) = refs[:-3], refs[-3:]
     frames = chunks.shape[0]
-    me = lax.axis_index("tm")
-    for piece, source in zip(arrived, sources):
-        if source is None:
-            for slot in range(frames):
-                chunks[owner[slot]] = piece[slot].astype(F32)
-        else:
-            chunks[owner[source(me)]] = piece[...].astype(F32)
+    if len(arrived) == frames:
+        pieces = [piece[...].astype(F32) for piece in arrived]
+    else:
+        pieces = [arrived[0][slot].astype(F32) for slot in range(frames)]
+    lines = pieces[0].shape[0]
+    for t in range(frames):
+        for dy in range(lines):
+            chosen = pieces[0][dy]
+            for slot in range(1, frames):
+                chosen = jnp.where(picks[slot] == t, pieces[slot][dy], chosen)
+            chunks[t, dy] = chosen
     cells = out.shape[3] // (PX * OUTC)
     stride = out.shape[1]
     held = chunks.shape[2]
     kept = up_to(cells, 8)
     lane = lax.broadcasted_iota(jnp.int32, (kept, LANES), 1)
     wide = PX * OUTC
-    shift = jnp.concatenate([bias[...]] * PX, axis=1)
+    shift = bias[0:1, :]
     pitch = folded.shape[1] // kept
     for line in range(stride):
         lines = []
@@ -322,7 +379,7 @@
     return ring(axis, way)
 
 
-def call(kernel, outs, specs, scratch, name, work=(0, 0)):
+def call(kernel, outs, specs, scratch, name, work=(0, 0), limit=16):
     return pl.pallas_call(
         kernel,
         out_shape=outs,
@@ -330,6 +387,7 @@
         out_specs=jax.tree.map(lambda _: vm(), outs),
         scratch_shapes=scratch,
         name=name,
+        compiler_params=pltpu.CompilerParams(vmem_limit_bytes=limit << 20),
         cost_estimate=pl.CostEstimate(flops=work[0], bytes_accessed=work[1], transcendentals=0),
     )
 
@@ -347,15 +405,16 @@
     band = shaped((4, lanes), BF16)
     column = shaped((2 * height, LANES), BF16)
     corner = shaped((4, LANES), BF16)
-    sends = call(
+    own, *sends = call(
         functools.partial(halo_kernel, row_dirs, col_dirs),
-        [band] * len(row_dirs)
+        [shaped(frames.shape, BF16)]
+        + [band] * len(row_dirs)
         + [column] * len(col_dirs)
         + [corner] * (len(row_dirs) * len(col_dirs)),
-        [vm(), sm()],
-        [VMEM((8, lanes), F32)],
+        [far(), far()],
+        [VMEM((8, lanes), F32), SMEM(valid_blocks.shape, jnp.int32), DMA((2,))],
         "halo",
-    )(frames, valid_blocks)
+    )(in_far(frames), in_far(valid_blocks))
     sends = iter(sends)
     by_row = {w: lax.ppermute(next(sends), "row", pairs_of("row", w)) for w in row_dirs}
     by_col = {w: lax.ppermute(next(sends), "col", pairs_of("col", w)) for w in col_dirs}
@@ -375,29 +434,30 @@
     def pick_both(w, v):
         return by_both[w if w in row_dirs else 0, v if v in col_dirs else 0]
 
-    filter_matrix = call(
-        filter_matrix_kernel,
-        shaped((12 * LANES, 2 * LANES), BF16),
-        [vm()],
-        [],
-        "filter_matrix",
-        (1 << 22, 1 << 20),
-    )(deblock_weight)
-    encoder_matrix = call(
-        encoder_matrix_kernel,
-        shaped((6 * LANES, 3 * PX * OUTC), BF16),
-        [vm()],
-        [],
-        "encoder_matrix",
-        (1 << 22, 1 << 20),
-    )(encoder_weight)
-
     rows = height // 2
     stride = rows // bands
     cells = lanes // LANES // 2 + 1
     held = up_to(rows + 2, 8)
     kept = up_to(cells, 8)
     piece = shaped((stride + 2, kept, LANES), BF16)
+    filter_matrix, filter_shift, masks = call(
+        functools.partial(filter_matrix_kernel, held),
+        [
+            shaped((12 * LANES, 2 * LANES), BF16),
+            shaped((8, LANES), F32),
+            shaped(((cells - 1) * held, LANES), F32),
+        ],
+        [far()] * 3,
+        [
+            VMEM((CH, 9 * CH), BF16),
+            VMEM((1, CH), F32),
+            SMEM(valid_blocks.shape, jnp.int32),
+            VMEM((LANES, up_to(9 * CH, LANES)), F32),
+            DMA((3,)),
+        ],
+        "filter_matrix",
+        (1 << 22, 1 << 20),
+    )(in_far(deblock_weight.T), in_far(deblock_bias.reshape(1, CH)), in_far(valid_blocks))
     direct = bands <= 4 and bands & (bands - 1) == 0
     if direct:
         order = [functools.partial(lambda k, me: me ^ k, k) for k in range(bands)]
@@ -406,7 +466,7 @@
     parts = call(
         functools.partial(pool_kernel, order, stride),
         [piece] * bands,
-        [vm(), sm()] + [vm()] * 10,
+        [vm()] * 12,
         [
             VMEM(((lanes // LANES + 2) * up_to(8 + 2 * held, 8), LANES), F32),
             VMEM((kept * held, LANES), F32),
@@ -414,8 +474,7 @@
         "pool",
         (1 << 22, 1 << 20),
     )(
-        frames,
-        valid_blocks,
+        own,
         pick(by_row, 1),
         pick(by_row, -1),
         pick(by_col, -1),
@@ -425,30 +484,47 @@
         pick_both(-1, -1),
         pick_both(-1, 1),
         filter_matrix,
-        deblock_bias.reshape(1, CH),
+        filter_shift,
+        masks,
     )
     if direct:
         arrived = [parts[0]] + [
             lax.ppermute(parts[k], "tm", [(i, i ^ k) for i in range(bands)])
-            for k in range(bands - 1, 0, -1)
+            for k in range(1, bands)
         ]
-        sources = [order[0]] + [order[k] for k in range(bands - 1, 0, -1)]
     else:
         arrived = [
             lax.all_to_all(jnp.stack(parts), "tm", split_axis=0, concat_axis=0, tiled=True)
         ]
-        sources = [None]
+    encoder_matrix, encoder_shift, picks = call(
+        functools.partial(encoder_matrix_kernel, order),
+        [
+            shaped((6 * LANES, 3 * PX * OUTC), BF16),
+            shaped((8, PX * OUTC), F32),
+            shaped((bands, kept, LANES), jnp.int32),
+        ],
+        [far()] * 3,
+        [
+            VMEM((OUTC, 27 * CH), BF16),
+            VMEM((1, OUTC), F32),
+            SMEM(owner_map.shape, jnp.int32),
+            VMEM((LANES, up_to(27 * CH, LANES)), F32),
+            DMA((3,)),
+        ],
+        "encoder_matrix",
+        (1 << 22, 1 << 20),
+    )(in_far(encoder_weight.T), in_far(encoder_bias.reshape(1, OUTC)), in_far(owner_map))
     encoded = call(
-        functools.partial(encode_kernel, sources),
+        encode_kernel,
         shaped((1, stride, bands - 1, lanes // 2 // CH * OUTC), BF16),
-        [sm(), vm(), vm()] + [vm()] * len(arrived),
+        [vm()] * (3 + len(arrived)),
         [
             VMEM((bands, stride + 2, kept, LANES), F32),
             VMEM((PX * OUTC // LANES, kept * up_to(bands - 1, 8), LANES), F32),
         ],
         "encode",
         (1 << 22, 1 << 20),
-    )(owner_map, encoder_matrix, encoder_bias.reshape(1, OUTC), *arrived)
+    )(encoder_matrix, encoder_shift, picks, *arrived)
     return encoded.transpose(2, 0, 1, 3)
 
 

time: 23.2 us -> 18.4 us (0.79)
  Pallas kernels: 10.3 us -> 4.46 us
  waiting for transfers between devices: 1.2 us -> 5.94 us
  local copies, waits for them, and re-layouts: 3.53 us -> 0 us
    pallas_call x4, Pallas kernels: 8.12 us -> 4.1 us  [the longest x1 1.13 us: on_device(): call(functools.partial(encoder_matrix_kernel, order), [shaped((6 * LANES,...]
    unnamed x16 -> x0, local copies, waits for them, and re-layouts: 3.53 us -> none
    ppermute x3, waiting for transfers between devices: 1.19 us -> 4.19 us  [on_device(): lax.ppermute(parts[k], 'tm', [(i, i ^ k) for i in range(bands)])]
    pallas_call x1, Pallas kernels: 2.17 us -> 0.37 us  [on_device(): call(functools.partial(pool_kernel, order, stride), [piece] * bands, [vm(...]
    ppermute x1, waiting for transfers between devices: 0.01 us -> 1.75 us  [on_device(): by_both[w, v] = lax.ppermute(next(sends), ('row', 'col'), pairs)]
    ppermute x3, starting transfers between devices: 4.77 us -> 4.45 us  [on_device(): lax.ppermute(parts[k], 'tm', [(i, i ^ k) for i in range(bands)])]
  transfers between devices with their start and end apart: 6 -> 6, of which waited for: 1 -> 3; matrix products, arithmetic and copies ran while one was open for 10% -> 0% of each run, Pallas kernels for 18% -> 12%
where the time goes in v2:
time: 18.4 us; the launch traced here: 18.1 us
  starting transfers between devices  7.68 us (42%)
  waiting for transfers between devices  5.94 us (32%)
  Pallas kernels  4.46 us (24%)
    ppermute x3, starting transfers between devices, on_device(): lax.ppermute(parts[k], 'tm', [(i, i ^ k) for i in range(bands)])  4.45 us
    ppermute x3, waiting for transfers between devices, on_device(): lax.ppermute(parts[k], 'tm', [(i, i ^ k) for i in range(bands)])  4.19 us
    ppermute x1, starting transfers between devices, on_device(): lax.ppermute(next(sends), 'row', pairs_of('row', w))  3.03 us
    ppermute x1, waiting for transfers between devices, on_device(): by_both[w, v] = lax.ppermute(next(sends), ('row', 'col'), pairs)  1.75 us
    pallas_call x1, Pallas kernels, on_device(): call(functools.partial(encoder_matrix_kernel, order), [shaped((6 * LANES,...  1.13 us
    pallas_call x1, Pallas kernels, on_device(): call(functools.partial(filter_matrix_kernel, held), [shaped((12 * LANES,...  1.05 us
    pallas_call x1, Pallas kernels, on_device(): call(encode_kernel, shaped((1, stride, bands - 1, lanes // 2 // CH * OUTC...  0.96 us
    pallas_call x1, Pallas kernels, on_device(): call(functools.partial(halo_kernel, row_dirs, col_dirs), [shaped(frames.s...  0.94 us
  transfers between devices with their start and end apart: 6, of which 3 were waited for; matrix products, arithmetic and copies ran while one was open for 0% of the time, Pallas kernels for 12%

profile of v2, /device:TPU:0, one launch (start us, length us, event | category | flops | bytes accessed | tf_op | source)
XLA Modules:
  0.0 18.1 jit_solution(5005560716708133862)
XLA Ops:
  0.0 0.9 %halo.1 = (bf16[1,8,4608]{2,1,0:T(8,128)(2,1)S(1)}, bf16[4,4608]{1,0:T(4,128)(2,1)S(1)}, bf16[16,128]{1,0:T(8,128)(2,1)S(1)}, bf16[4,128]{1,0:T(4,128)(2,1)S(1)}) custom-call(bf16[1,8,4608]{2,1,0:T(8,128)(2,1)} %frames_far.1, s32[1,1,18]{2,1,0:T(1,128)} %valid_far.3), custom_call_target="tpu_custom_call" | custom-call | tf_op jit(solution)/shard_map/halo/pallas_call | solution.py:408
  1.0 3.0 %collective-permute-start = (bf16[4,4608]{1,0:T(4,128)(2,1)S(1)}, bf16[4,4608]{1,0:T(4,128)(2,1)S(1)}, u32[]{:S(2)}, u32[]{:S(2)}) collective-permute-start(bf16[4,4608]{1,0:T(4,128)(2,1)S(1)} %get-tuple-element.23), channel_id=1, source_target_pairs={{0,2},{2,0},{1,3},{3,1},{4,6},{6,4},{5,7},{7,5},{8,10},{10,8},{9,1... | collective-permute-start | bytes 110600 | tf_op jit(solution)/shard_map/ppermute | solution.py:419
  4.0 0.0 collective-permute-start.1
  4.0 0.2 %collective-permute-start.2 = (bf16[4,128]{1,0:T(4,128)(2,1)S(1)}, bf16[4,128]{1,0:T(4,128)(2,1)S(1)}, u32[]{:S(2)}, u32[]{:S(2)}) collective-permute-start(bf16[4,128]{1,0:T(4,128)(2,1)S(1)} %get-tuple-element.25), channel_id=1, source_target_pairs={{0,3},{1,2},{2,1},{3,0},{4,7},{5,6},{6,5},{7,4},{8,11},{9,10},{10,... | collective-permute-start | bytes 3080 | tf_op jit(solution)/shard_map/ppermute | solution.py:429
  4.2 1.1 %filter_matrix.1 = (bf16[1536,256]{1,0:T(8,128)(2,1)S(1)}, f32[8,128]{1,0:T(8,128)S(1)}, f32[144,128]{1,0:T(8,128)S(1)}) custom-call(bf16[32,288]{1,0:T(8,128)(2,1)} %bitcast.6, f32[1,32]{1,0:T(1,128)} %bitcast.8, s32[1,1,18]{2,1,0:T(1,128)} %valid_far.3), custom_call_target="tpu_custom_call" | custom-call | flops 4194304 | bytes 1048576 | tf_op jit(solution)/shard_map/filter_matrix/pallas_call | solution.py:443
  5.2 1.7 %collective-permute-done.2.ur.ul.dr.dl = bf16[4,128]{1,0:T(4,128)(2,1)S(1)} collective-permute-done((bf16[4,128]{1,0:T(4,128)(2,1)S(1)}, bf16[4,128]{1,0:T(4,128)(2,1)S(1)}, u32[]{:S(2)}, u32[]{:S(2)}) %collective-permute-start.2) | collective-permute-done | bytes 1056 | tf_op jit(solution)/shard_map/ppermute | solution.py:429
  7.0 0.0 collective-permute-done.1.rt.lf
  7.0 0.0 collective-permute-done.up.dn
  7.0 0.4 %pool.1 = (bf16[3,24,128]{2,1,0:T(8,128)(2,1)S(1)}, bf16[3,24,128]{2,1,0:T(8,128)(2,1)S(1)}, bf16[3,24,128]{2,1,0:T(8,128)(2,1)S(1)}, bf16[3,24,128]{2,1,0:T(8,128)(2,1)S(1)}) custom-call(bf16[1,8,4608]{2,1,0:T(8,128)(2,1)S(1)} %get-tuple-element.22.frames, bf16[4,4608]{1,0:T(4,128)(2,1)S(1)} %collective-permute-done.up.dn, ...), custom_call_target="tpu_custom_call" | custom-call | flops 4194304 | bytes 1048576 | tf_op jit(solution)/shard_map/pool/pallas_call | solution.py:466
  7.4 1.6 %collective-permute-start.3 = (bf16[3,24,128]{2,1,0:T(8,128)(2,1)S(1)}, bf16[3,24,128]{2,1,0:T(8,128)(2,1)S(1)}, u32[]{:S(2)}, u32[]{:S(2)}) collective-permute-start(bf16[3,24,128]{2,1,0:T(8,128)(2,1)S(1)} %get-tuple-element.30), channel_id=1, source_target_pairs={{0,4},{4,0},{8,12},{12,8},{1,5},{5,1},{9,13},{13,9},{2,6},{6,2},{1... | collective-permute-start | bytes 55304 | tf_op jit(solution)/shard_map/ppermute | solution.py:492
  9.0 2.6 %collective-permute-start.4 = (bf16[3,24,128]{2,1,0:T(8,128)(2,1)S(1)}, bf16[3,24,128]{2,1,0:T(8,128)(2,1)S(1)}, u32[]{:S(2)}, u32[]{:S(2)}) collective-permute-start(bf16[3,24,128]{2,1,0:T(8,128)(2,1)S(1)} %get-tuple-element.31), channel_id=1, source_target_pairs={{0,8},{4,12},{8,0},{12,4},{1,9},{5,13},{9,1},{13,5},{2,10},{6,14},... | collective-permute-start | bytes 55304 | tf_op jit(solution)/shard_map/ppermute | solution.py:492
  11.6 0.2 %collective-permute-start.5 = (bf16[3,24,128]{2,1,0:T(8,128)(2,1)S(1)}, bf16[3,24,128]{2,1,0:T(8,128)(2,1)S(1)}, u32[]{:S(2)}, u32[]{:S(2)}) collective-permute-start(bf16[3,24,128]{2,1,0:T(8,128)(2,1)S(1)} %get-tuple-element.32), channel_id=1, source_target_pairs={{0,12},{4,8},{8,4},{12,0},{1,13},{5,9},{9,5},{13,1},{2,14},{6,10},... | collective-permute-start | bytes 55304 | tf_op jit(solution)/shard_map/ppermute | solution.py:492
  11.8 1.1 %encoder_matrix.1 = (bf16[768,768]{1,0:T(8,128)(2,1)S(1)}, f32[8,256]{1,0:T(8,128)S(1)}, s32[4,24,128]{2,1,0:T(8,128)S(1)}) custom-call(bf16[64,864]{1,0:T(8,128)(2,1)} %bitcast.5, f32[1,64]{1,0:T(1,128)} %bitcast.7, s32[4]{0:T(128)} %owner_far.1), custom_call_target="tpu_custom_call" | custom-call | flops 4194304 | bytes 1048576 | tf_op jit(solution)/shard_map/encoder_matrix/pallas_call | solution.py:499
  13.0 0.0 collective-permute-done.3.refs_1_
  13.0 0.8 %collective-permute-done.4.refs_2_ = bf16[3,24,128]{2,1,0:T(8,128)(2,1)S(1)} collective-permute-done((bf16[3,24,128]{2,1,0:T(8,128)(2,1)S(1)}, bf16[3,24,128]{2,1,0:T(8,128)(2,1)S(1)}, u32[]{:S(2)}, u32[]{:S(2)}) %collective-permute-start.4) | collective-permute-done | bytes 18464 | tf_op jit(solution)/shard_map/ppermute | solution.py:492
  13.8 3.4 %collective-permute-done.5.refs_3_ = bf16[3,24,128]{2,1,0:T(8,128)(2,1)S(1)} collective-permute-done((bf16[3,24,128]{2,1,0:T(8,128)(2,1)S(1)}, bf16[3,24,128]{2,1,0:T(8,128)(2,1)S(1)}, u32[]{:S(2)}, u32[]{:S(2)}) %collective-permute-start.5) | collective-permute-done | bytes 18464 | tf_op jit(solution)/shard_map/ppermute | solution.py:492
  17.2 1.0 %encode.1 = bf16[1,1,3,4608]{3,2,1,0:T(4,128)(2,1)} custom-call(bf16[768,768]{1,0:T(8,128)(2,1)S(1)} %get-tuple-element.19.matrix, f32[8,256]{1,0:T(8,128)S(1)} %get-tuple-element.20.bias, s32[4,24,128]{2,1,0:T(8,128)S(1)} %get-tuple-element.21.picks, bf16[3,24,128]{2,1,0:T(8,128)(2,1)S(1)} %get-tuple-element.29.refs_0_, ...), custom_call_target="tpu_custom_call" | custom-call | flops 4194304 | bytes 1048576 | tf_op jit(solution)/shard_map/encode/pallas_call | solution.py:517
Async XLA Ops:
  1.0 6.0 %collective-permute-start = (bf16[4,4608]{1,0:T(4,128)(2,1)S(1)}, bf16[4,4608]{1,0:T(4,128)(2,1)S(1)}, u32[]{:S(2)}, u32[]{:S(2)}) collective-permute-start(bf16[4,4608]{1,0:T(4,128)(2,1)S(1)} %get-tuple-element.23), channel_id=1, source_target_pairs={{0,2},{2,0},{1,3},{3,1},{4,6},{6,4},{5,7},{7,5},{8,10},{10,8},{9,1... | collective-permute-start | bytes 110600 | tf_op jit(solution)/shard_map/ppermute | solution.py:419
  4.0 3.0 %collective-permute-start.1 = (bf16[16,128]{1,0:T(8,128)(2,1)S(1)}, bf16[16,128]{1,0:T(8,128)(2,1)S(1)}, u32[]{:S(2)}, u32[]{:S(2)}) collective-permute-start(bf16[16,128]{1,0:T(8,128)(2,1)S(1)} %get-tuple-element.24), channel_id=1, source_target_pairs={{0,1},{1,0},{2,3},{3,2},{4,5},{5,4},{6,7},{7,6},{8,9},{9,8},{10,11... | collective-permute-start | bytes 12296 | tf_op jit(solution)/shard_map/ppermute | solution.py:420
  4.0 3.0 %collective-permute-start.2 = (bf16[4,128]{1,0:T(4,128)(2,1)S(1)}, bf16[4,128]{1,0:T(4,128)(2,1)S(1)}, u32[]{:S(2)}, u32[]{:S(2)}) collective-permute-start(bf16[4,128]{1,0:T(4,128)(2,1)S(1)} %get-tuple-element.25), channel_id=1, source_target_pairs={{0,3},{1,2},{2,1},{3,0},{4,7},{5,6},{6,5},{7,4},{8,11},{9,10},{10,... | collective-permute-start | bytes 3080 | tf_op jit(solution)/shard_map/ppermute | solution.py:429
  7.4 5.6 %collective-permute-start.3 = (bf16[3,24,128]{2,1,0:T(8,128)(2,1)S(1)}, bf16[3,24,128]{2,1,0:T(8,128)(2,1)S(1)}, u32[]{:S(2)}, u32[]{:S(2)}) collective-permute-start(bf16[3,24,128]{2,1,0:T(8,128)(2,1)S(1)} %get-tuple-element.30), channel_id=1, source_target_pairs={{0,4},{4,0},{8,12},{12,8},{1,5},{5,1},{9,13},{13,9},{2,6},{6,2},{1... | collective-permute-start | bytes 55304 | tf_op jit(solution)/shard_map/ppermute | solution.py:492
  9.0 4.7 %collective-permute-start.4 = (bf16[3,24,128]{2,1,0:T(8,128)(2,1)S(1)}, bf16[3,24,128]{2,1,0:T(8,128)(2,1)S(1)}, u32[]{:S(2)}, u32[]{:S(2)}) collective-permute-start(bf16[3,24,128]{2,1,0:T(8,128)(2,1)S(1)} %get-tuple-element.31), channel_id=1, source_target_pairs={{0,8},{4,12},{8,0},{12,4},{1,9},{5,13},{9,1},{13,5},{2,10},{6,14},... | collective-permute-start | bytes 55304 | tf_op jit(solution)/shard_map/ppermute | solution.py:492
  11.6 5.6 %collective-permute-start.5 = (bf16[3,24,128]{2,1,0:T(8,128)(2,1)S(1)}, bf16[3,24,128]{2,1,0:T(8,128)(2,1)S(1)}, u32[]{:S(2)}, u32[]{:S(2)}) collective-permute-start(bf16[3,24,128]{2,1,0:T(8,128)(2,1)S(1)} %get-tuple-element.32), channel_id=1, source_target_pairs={{0,12},{4,8},{8,4},{12,0},{1,13},{5,9},{9,5},{13,1},{2,14},{6,10},... | collective-permute-start | bytes 55304 | tf_op jit(solution)/shard_map/ppermute | solution.py:492

commit v3 on v2

--- a/solution.py
+++ b/solution.py
@@ -120,12 +120,18 @@
     )
 
 
-def filter_matrix_kernel(
-    held, weight_far, bias_far, valid_far, out, shift, masks, weight, bias, valid, staged, sems
-):
-    copies = fetch((weight_far, weight), (bias_far, bias), (valid_far, valid), sems)
+def prepare_kernel(held, sources, *refs):
+    far_refs, refs = refs[:6], refs[6:]
+    filter_outs, encoder_outs, refs = refs[:3], refs[3:6], refs[6:]
+    near_refs, (filter_staged, encoder_staged, sems) = refs[:6], refs[6:]
+    copies = fetch(*zip(far_refs, near_refs), sems)
     for copy in copies:
         copy.wait()
+    filter_matrix(held, *filter_outs, *near_refs[:3], filter_staged)
+    encoder_matrix(sources, *encoder_outs, *near_refs[3:], encoder_staged)
+
+
+def filter_matrix(held, out, shift, masks, weight, bias, valid, staged):
     shift[...] = jnp.broadcast_to(jnp.concatenate([bias[...]] * PX, axis=1), shift.shape)
     spots = lax.broadcasted_iota(jnp.int32, (held, LANES), 0)
     for c in range(valid.shape[2]):
@@ -169,12 +175,7 @@
         out[spot : spot + LANES - 2 * CH, :] = jnp.zeros((LANES - 2 * CH, 2 * LANES), BF16)
 
 
-def encoder_matrix_kernel(
-    sources, weight_far, bias_far, owner_far, out, shift, picks, weight, bias, owner, staged, sems
-):
-    copies = fetch((weight_far, weight), (bias_far, bias), (owner_far, owner), sems)
-    for copy in copies:
-        copy.wait()
+def encoder_matrix(sources, out, shift, picks, weight, bias, owner, staged):
     shift[...] = jnp.broadcast_to(jnp.concatenate([bias[...]] * PX, axis=1), shift.shape)
     me = lax.axis_index("tm")
     for spot, source in enumerate(sources):
@@ -379,14 +380,13 @@
     return ring(axis, way)
 
 
-def call(kernel, outs, specs, scratch, name, work=(0, 0), limit=16):
+def call(kernel, outs, specs, scratch, work=(0, 0), limit=16):
     return pl.pallas_call(
         kernel,
         out_shape=outs,
         in_specs=specs,
         out_specs=jax.tree.map(lambda _: vm(), outs),
         scratch_shapes=scratch,
-        name=name,
         compiler_params=pltpu.CompilerParams(vmem_limit_bytes=limit << 20),
         cost_estimate=pl.CostEstimate(flops=work[0], bytes_accessed=work[1], transcendentals=0),
     )
@@ -413,11 +413,13 @@
         + [corner] * (len(row_dirs) * len(col_dirs)),
         [far(), far()],
         [VMEM((8, lanes), F32), SMEM(valid_blocks.shape, jnp.int32), DMA((2,))],
-        "halo",
     )(in_far(frames), in_far(valid_blocks))
     sends = iter(sends)
-    by_row = {w: lax.ppermute(next(sends), "row", pairs_of("row", w)) for w in row_dirs}
-    by_col = {w: lax.ppermute(next(sends), "col", pairs_of("col", w)) for w in col_dirs}
+    by_row, by_col = {}, {}
+    for w in row_dirs:
+        by_row[w] = lax.ppermute(next(sends), "row", pairs_of("row", w))
+    for w in col_dirs:
+        by_col[w] = lax.ppermute(next(sends), "col", pairs_of("col", w))
     by_both = {}
     for w in row_dirs:
         for v in col_dirs:
@@ -440,29 +442,47 @@
     held = up_to(rows + 2, 8)
     kept = up_to(cells, 8)
     piece = shaped((stride + 2, kept, LANES), BF16)
-    filter_matrix, filter_shift, masks = call(
-        functools.partial(filter_matrix_kernel, held),
+    direct = bands <= 4
+    if direct:
+        order = [functools.partial(lambda k, me: lax.rem(me + k, bands), k) for k in range(bands)]
+        sources = [
+            functools.partial(lambda k, me: lax.rem(me + bands - k, bands), k)
+            for k in range(bands)
+        ]
+    else:
+        order = [functools.partial(lambda k, me: k, k) for k in range(bands)]
+        sources = order
+    filter_table, filter_shift, masks, encoder_table, encoder_shift, picks = call(
+        functools.partial(prepare_kernel, held, sources),
         [
             shaped((12 * LANES, 2 * LANES), BF16),
             shaped((8, LANES), F32),
             shaped(((cells - 1) * held, LANES), F32),
+            shaped((6 * LANES, 3 * PX * OUTC), BF16),
+            shaped((8, PX * OUTC), F32),
+            shaped((bands, kept, LANES), jnp.int32),
         ],
-        [far()] * 3,
+        [far()] * 6,
         [
             VMEM((CH, 9 * CH), BF16),
             VMEM((1, CH), F32),
             SMEM(valid_blocks.shape, jnp.int32),
+            VMEM((OUTC, 27 * CH), BF16),
+            VMEM((1, OUTC), F32),
+            SMEM(owner_map.shape, jnp.int32),
             VMEM((LANES, up_to(9 * CH, LANES)), F32),
-            DMA((3,)),
+            VMEM((LANES, up_to(27 * CH, LANES)), F32),
+            DMA((6,)),
         ],
-        "filter_matrix",
         (1 << 22, 1 << 20),
-    )(in_far(deblock_weight.T), in_far(deblock_bias.reshape(1, CH)), in_far(valid_blocks))
-    direct = bands <= 4 and bands & (bands - 1) == 0
-    if direct:
-        order = [functools.partial(lambda k, me: me ^ k, k) for k in range(bands)]
-    else:
-        order = [functools.partial(lambda k, me: k, k) for k in range(bands)]
+    )(
+        in_far(deblock_weight.T),
+        in_far(deblock_bias.reshape(1, CH)),
+        in_far(valid_blocks),
+        in_far(encoder_weight.T),
+        in_far(encoder_bias.reshape(1, OUTC)),
+        in_far(owner_map),
+    )
     parts = call(
         functools.partial(pool_kernel, order, stride),
         [piece] * bands,
@@ -471,7 +491,6 @@
             VMEM(((lanes // LANES + 2) * up_to(8 + 2 * held, 8), LANES), F32),
             VMEM((kept * held, LANES), F32),
         ],
-        "pool",
         (1 << 22, 1 << 20),
     )(
         own,
@@ -483,37 +502,19 @@
         pick_both(1, 1),
         pick_both(-1, -1),
         pick_both(-1, 1),
-        filter_matrix,
+        filter_table,
         filter_shift,
         masks,
     )
     if direct:
-        arrived = [parts[0]] + [
-            lax.ppermute(parts[k], "tm", [(i, i ^ k) for i in range(bands)])
-            for k in range(1, bands)
-        ]
+        arrived = [parts[0]]
+        for k in range(1, bands):
+            pairs = [(i, (i + k) % bands) for i in range(bands)]
+            arrived.append(lax.ppermute(parts[k], "tm", pairs))
     else:
         arrived = [
             lax.all_to_all(jnp.stack(parts), "tm", split_axis=0, concat_axis=0, tiled=True)
         ]
-    encoder_matrix, encoder_shift, picks = call(
-        functools.partial(encoder_matrix_kernel, order),
-        [
-            shaped((6 * LANES, 3 * PX * OUTC), BF16),
-            shaped((8, PX * OUTC), F32),
-            shaped((bands, kept, LANES), jnp.int32),
-        ],
-        [far()] * 3,
-        [
-            VMEM((OUTC, 27 * CH), BF16),
-            VMEM((1, OUTC), F32),
-            SMEM(owner_map.shape, jnp.int32),
-            VMEM((LANES, up_to(27 * CH, LANES)), F32),
-            DMA((3,)),
-        ],
-        "encoder_matrix",
-        (1 << 22, 1 << 20),
-    )(in_far(encoder_weight.T), in_far(encoder_bias.reshape(1, OUTC)), in_far(owner_map))
     encoded = call(
         encode_kernel,
         shaped((1, stride, bands - 1, lanes // 2 // CH * OUTC), BF16),
@@ -522,9 +523,8 @@
             VMEM((bands, stride + 2, kept, LANES), F32),
             VMEM((PX * OUTC // LANES, kept * up_to(bands - 1, 8), LANES), F32),
         ],
-        "encode",
         (1 << 22, 1 << 20),
-    )(encoder_matrix, encoder_shift, picks, *arrived)
+    )(encoder_table, encoder_shift, picks, *arrived)
     return encoded.transpose(2, 0, 1, 3)
 
 

time: 18.4 us -> 16.5 us (0.90)
  waiting for transfers between devices: 5.94 us -> 3.85 us
  starting transfers between devices: 7.68 us -> 8.79 us
  Pallas kernels: 4.46 us -> 3.64 us
    ppermute x5, waiting for transfers between devices: 4.19 us -> 2.42 us  [the longest x3 2.41 us: on_device(): arrived.append(lax.ppermute(parts[k], 'tm', pairs))]
    ppermute x5, starting transfers between devices: 7.49 us -> 8.6 us  [the longest x3 5.56 us: on_device(): arrived.append(lax.ppermute(parts[k], 'tm', pairs))]
    pallas_call x2 -> x1, Pallas kernels: 2.19 us -> 1.37 us  [on_device(): call(functools.partial(prepare_kernel, held, sources), [shaped((12 * LANE...]
    ppermute x1, waiting for transfers between devices: 1.75 us -> 1.43 us  [on_device(): by_both[w, v] = lax.ppermute(next(sends), ('row', 'col'), pairs)]
  transfers between devices with their start and end apart: 6 -> 6, of which waited for: 3 -> 4; matrix products, arithmetic and copies ran while one was open for 0% -> 0% of each run, Pallas kernels for 12% -> 8%
where the time goes in v3:
time: 16.5 us; the launch traced here: 16.3 us
  starting transfers between devices  8.79 us (53%)
  waiting for transfers between devices  3.85 us (23%)
  Pallas kernels  3.64 us (22%)
    ppermute x3, starting transfers between devices, on_device(): arrived.append(lax.ppermute(parts[k], 'tm', pairs))  5.56 us
    ppermute x1, starting transfers between devices, on_device(): by_row[w] = lax.ppermute(next(sends), 'row', pairs_of('row', w))  3.03 us
    ppermute x3, waiting for transfers between devices, on_device(): arrived.append(lax.ppermute(parts[k], 'tm', pairs))  2.41 us
    ppermute x1, waiting for transfers between devices, on_device(): by_both[w, v] = lax.ppermute(next(sends), ('row', 'col'), pairs)  1.43 us
    pallas_call x1, Pallas kernels, on_device(): call(functools.partial(prepare_kernel, held, sources), [shaped((12 * LANE...  1.37 us
    pallas_call x1, Pallas kernels, on_device(): call(encode_kernel, shaped((1, stride, bands - 1, lanes // 2 // CH * OUTC...  0.97 us
    pallas_call x1, Pallas kernels, on_device(): call(functools.partial(halo_kernel, row_dirs, col_dirs), [shaped(frames.s...  0.94 us
    pallas_call x1, Pallas kernels, on_device(): call(functools.partial(pool_kernel, order, stride), [piece] * bands, [vm(...  0.36 us
  transfers between devices with their start and end apart: 6, of which 4 were waited for; matrix products, arithmetic and copies ran while one was open for 0% of the time, Pallas kernels for 8%

profile of v3, /device:TPU:0, one launch (start us, length us, event | category | flops | bytes accessed | tf_op | source)
XLA Modules:
  0.0 16.3 jit_solution(1782955094200417502)
XLA Ops:
  0.0 0.9 %shard_map.74 = (bf16[1,8,4608]{2,1,0:T(8,128)(2,1)S(1)}, bf16[4,4608]{1,0:T(4,128)(2,1)S(1)}, bf16[16,128]{1,0:T(8,128)(2,1)S(1)}, bf16[4,128]{1,0:T(4,128)(2,1)S(1)}) custom-call(bf16[1,8,4608]{2,1,0:T(8,128)(2,1)} %frames_far.1, s32[1,1,18]{2,1,0:T(1,128)} %valid_far.1), custom_call_target="tpu_custom_call" | custom-call | tf_op jit(solution)/shard_map/pallas_call | solution.py:408
  1.0 3.0 %collective-permute-start = (bf16[4,4608]{1,0:T(4,128)(2,1)S(1)}, bf16[4,4608]{1,0:T(4,128)(2,1)S(1)}, u32[]{:S(2)}, u32[]{:S(2)}) collective-permute-start(bf16[4,4608]{1,0:T(4,128)(2,1)S(1)} %get-tuple-element.23), channel_id=1, source_target_pairs={{0,2},{2,0},{1,3},{3,1},{4,6},{6,4},{5,7},{7,5},{8,10},{10,8},{9,1... | collective-permute-start | bytes 110600 | tf_op jit(solution)/shard_map/ppermute | solution.py:420
  4.0 0.0 collective-permute-start.1
  4.0 0.2 %collective-permute-start.2 = (bf16[4,128]{1,0:T(4,128)(2,1)S(1)}, bf16[4,128]{1,0:T(4,128)(2,1)S(1)}, u32[]{:S(2)}, u32[]{:S(2)}) collective-permute-start(bf16[4,128]{1,0:T(4,128)(2,1)S(1)} %get-tuple-element.25), channel_id=1, source_target_pairs={{0,3},{1,2},{2,1},{3,0},{4,7},{5,6},{6,5},{7,4},{8,11},{9,10},{10,... | collective-permute-start | bytes 3080 | tf_op jit(solution)/shard_map/ppermute | solution.py:431
  4.2 1.4 %shard_map.73 = (bf16[1536,256]{1,0:T(8,128)(2,1)S(1)}, f32[8,128]{1,0:T(8,128)S(1)}, f32[144,128]{1,0:T(8,128)S(1)}, bf16[768,768]{1,0:T(8,128)(2,1)S(1)}, f32[...) custom-call(bf16[32,288]{1,0:T(8,128)(2,1)} %bitcast.6, f32[1,32]{1,0:T(1,128)} %bitcast.7, s32[1,1,18]{2,1,0:T(1,128)} %valid_far.1, ...), custom_call_target="tpu_custom_call" | custom-call | flops 4194304 | bytes 1048576 | tf_op jit(solution)/shard_map/pallas_call | solution.py:455
  5.6 1.4 %collective-permute-done.2.ur.ul.dr.dl = bf16[4,128]{1,0:T(4,128)(2,1)S(1)} collective-permute-done((bf16[4,128]{1,0:T(4,128)(2,1)S(1)}, bf16[4,128]{1,0:T(4,128)(2,1)S(1)}, u32[]{:S(2)}, u32[]{:S(2)}) %collective-permute-start.2) | collective-permute-done | bytes 1056 | tf_op jit(solution)/shard_map/ppermute | solution.py:431
  7.0 0.0 collective-permute-done.1.rt.lf
  7.0 0.0 collective-permute-done.up.dn
  7.0 0.4 %shard_map.75 = (bf16[3,24,128]{2,1,0:T(8,128)(2,1)S(1)}, bf16[3,24,128]{2,1,0:T(8,128)(2,1)S(1)}, bf16[3,24,128]{2,1,0:T(8,128)(2,1)S(1)}, bf16[3,24,128]{2,1,0:T(8,128)(2,1)S(1)}) custom-call(bf16[1,8,4608]{2,1,0:T(8,128)(2,1)S(1)} %get-tuple-element.22.frames, bf16[4,4608]{1,0:T(4,128)(2,1)S(1)} %collective-permute-done.up.dn, ...), custom_call_target="tpu_custom_call" | custom-call | flops 4194304 | bytes 1048576 | tf_op jit(solution)/shard_map/pallas_call | solution.py:486
  7.4 1.6 %collective-permute-start.3 = (bf16[3,24,128]{2,1,0:T(8,128)(2,1)S(1)}, bf16[3,24,128]{2,1,0:T(8,128)(2,1)S(1)}, u32[]{:S(2)}, u32[]{:S(2)}) collective-permute-start(bf16[3,24,128]{2,1,0:T(8,128)(2,1)S(1)} %get-tuple-element.30), channel_id=1, source_target_pairs={{0,4},{4,8},{8,12},{12,0},{1,5},{5,9},{9,13},{13,1},{2,6},{6,10},{... | collective-permute-start | bytes 55304 | tf_op jit(solution)/shard_map/ppermute | solution.py:513
  9.0 2.6 %collective-permute-start.4 = (bf16[3,24,128]{2,1,0:T(8,128)(2,1)S(1)}, bf16[3,24,128]{2,1,0:T(8,128)(2,1)S(1)}, u32[]{:S(2)}, u32[]{:S(2)}) collective-permute-start(bf16[3,24,128]{2,1,0:T(8,128)(2,1)S(1)} %get-tuple-element.31), channel_id=1, source_target_pairs={{0,8},{4,12},{8,0},{12,4},{1,9},{5,13},{9,1},{13,5},{2,10},{6,14},... | collective-permute-start | bytes 55304 | tf_op jit(solution)/shard_map/ppermute | solution.py:513
  11.6 1.3 %collective-permute-start.5 = (bf16[3,24,128]{2,1,0:T(8,128)(2,1)S(1)}, bf16[3,24,128]{2,1,0:T(8,128)(2,1)S(1)}, u32[]{:S(2)}, u32[]{:S(2)}) collective-permute-start(bf16[3,24,128]{2,1,0:T(8,128)(2,1)S(1)} %get-tuple-element.32), channel_id=1, source_target_pairs={{0,12},{4,0},{8,4},{12,8},{1,13},{5,1},{9,5},{13,9},{2,14},{6,2},{... | collective-permute-start | bytes 55304 | tf_op jit(solution)/shard_map/ppermute | solution.py:513
  12.9 0.1 collective-permute-done.3.refs_1_
  13.1 0.6 %collective-permute-done.4.refs_2_ = bf16[3,24,128]{2,1,0:T(8,128)(2,1)S(1)} collective-permute-done((bf16[3,24,128]{2,1,0:T(8,128)(2,1)S(1)}, bf16[3,24,128]{2,1,0:T(8,128)(2,1)S(1)}, u32[]{:S(2)}, u32[]{:S(2)}) %collective-permute-start.4) | collective-permute-done | bytes 18464 | tf_op jit(solution)/shard_map/ppermute | solution.py:513
  13.7 1.7 %collective-permute-done.5.refs_3_ = bf16[3,24,128]{2,1,0:T(8,128)(2,1)S(1)} collective-permute-done((bf16[3,24,128]{2,1,0:T(8,128)(2,1)S(1)}, bf16[3,24,128]{2,1,0:T(8,128)(2,1)S(1)}, u32[]{:S(2)}, u32[]{:S(2)}) %collective-permute-start.5) | collective-permute-done | bytes 18464 | tf_op jit(solution)/shard_map/ppermute | solution.py:513
  15.3 1.0 %shard_map.76 = bf16[1,1,3,4608]{3,2,1,0:T(4,128)(2,1)} custom-call(bf16[768,768]{1,0:T(8,128)(2,1)S(1)} %get-tuple-element.19.matrix, f32[8,256]{1,0:T(8,128)S(1)} %get-tuple-element.20.bias, s32[4,24,128]{2,1,0:T(8,128)S(1)} %get-tuple-element.21.picks, bf16[3,24,128]{2,1,0:T(8,128)(2,1)S(1)} %get-tuple-element.29.refs_0_, ...), custom_call_target="tpu_custom_call" | custom-call | flops 4194304 | bytes 1048576 | tf_op jit(solution)/shard_map/pallas_call | solution.py:518
Async XLA Ops:
  1.0 6.0 %collective-permute-start = (bf16[4,4608]{1,0:T(4,128)(2,1)S(1)}, bf16[4,4608]{1,0:T(4,128)(2,1)S(1)}, u32[]{:S(2)}, u32[]{:S(2)}) collective-permute-start(bf16[4,4608]{1,0:T(4,128)(2,1)S(1)} %get-tuple-element.23), channel_id=1, source_target_pairs={{0,2},{2,0},{1,3},{3,1},{4,6},{6,4},{5,7},{7,5},{8,10},{10,8},{9,1... | collective-permute-start | bytes 110600 | tf_op jit(solution)/shard_map/ppermute | solution.py:420
  4.0 3.0 %collective-permute-start.1 = (bf16[16,128]{1,0:T(8,128)(2,1)S(1)}, bf16[16,128]{1,0:T(8,128)(2,1)S(1)}, u32[]{:S(2)}, u32[]{:S(2)}) collective-permute-start(bf16[16,128]{1,0:T(8,128)(2,1)S(1)} %get-tuple-element.24), channel_id=1, source_target_pairs={{0,1},{1,0},{2,3},{3,2},{4,5},{5,4},{6,7},{7,6},{8,9},{9,8},{10,11... | collective-permute-start | bytes 12296 | tf_op jit(solution)/shard_map/ppermute | solution.py:422
  4.0 3.0 %collective-permute-start.2 = (bf16[4,128]{1,0:T(4,128)(2,1)S(1)}, bf16[4,128]{1,0:T(4,128)(2,1)S(1)}, u32[]{:S(2)}, u32[]{:S(2)}) collective-permute-start(bf16[4,128]{1,0:T(4,128)(2,1)S(1)} %get-tuple-element.25), channel_id=1, source_target_pairs={{0,3},{1,2},{2,1},{3,0},{4,7},{5,6},{6,5},{7,4},{8,11},{9,10},{10,... | collective-permute-start | bytes 3080 | tf_op jit(solution)/shard_map/ppermute | solution.py:431
  7.4 5.7 %collective-permute-start.3 = (bf16[3,24,128]{2,1,0:T(8,128)(2,1)S(1)}, bf16[3,24,128]{2,1,0:T(8,128)(2,1)S(1)}, u32[]{:S(2)}, u32[]{:S(2)}) collective-permute-start(bf16[3,24,128]{2,1,0:T(8,128)(2,1)S(1)} %get-tuple-element.30), channel_id=1, source_target_pairs={{0,4},{4,8},{8,12},{12,0},{1,5},{5,9},{9,13},{13,1},{2,6},{6,10},{... | collective-permute-start | bytes 55304 | tf_op jit(solution)/shard_map/ppermute | solution.py:513
  9.0 4.7 %collective-permute-start.4 = (bf16[3,24,128]{2,1,0:T(8,128)(2,1)S(1)}, bf16[3,24,128]{2,1,0:T(8,128)(2,1)S(1)}, u32[]{:S(2)}, u32[]{:S(2)}) collective-permute-start(bf16[3,24,128]{2,1,0:T(8,128)(2,1)S(1)} %get-tuple-element.31), channel_id=1, source_target_pairs={{0,8},{4,12},{8,0},{12,4},{1,9},{5,13},{9,1},{13,5},{2,10},{6,14},... | collective-permute-start | bytes 55304 | tf_op jit(solution)/shard_map/ppermute | solution.py:513
  11.6 3.8 %collective-permute-start.5 = (bf16[3,24,128]{2,1,0:T(8,128)(2,1)S(1)}, bf16[3,24,128]{2,1,0:T(8,128)(2,1)S(1)}, u32[]{:S(2)}, u32[]{:S(2)}) collective-permute-start(bf16[3,24,128]{2,1,0:T(8,128)(2,1)S(1)} %get-tuple-element.32), channel_id=1, source_target_pairs={{0,12},{4,0},{8,4},{12,8},{1,13},{5,1},{9,5},{13,9},{2,14},{6,2},{... | collective-permute-start | bytes 55304 | tf_op jit(solution)/shard_map/ppermute | solution.py:513

commit v4 on v3

--- a/solution.py
+++ b/solution.py
@@ -56,8 +56,8 @@
     return (0,) if lax.axis_size(axis) <= 2 else (1, -1)
 
 
-def halo_kernel(row_dirs, col_dirs, frames_far, valid_far, frames, *refs):
-    sends, (marks, valid, sems) = refs[:-3], refs[-3:]
+def halo_kernel(row_dirs, col_dirs, frames_far, valid_far, tile, *refs):
+    sends, (frames, marks, valid, sems) = refs[:-4], refs[-4:]
     whole, flags = fetch((frames_far, frames), (valid_far, valid), sems)
     flags.wait()
     height = frames.shape[1]
@@ -65,18 +65,21 @@
     blocks = valid.shape[2]
     last = valid.shape[1] - 1
     wide = lanes // blocks
-    for block in range(blocks):
-        window = pl.ds(block * wide, wide)
-        for spot, line in ((0, last), (3, 0)):
-            marks[spot : spot + 1, window] = jnp.full(
+    if last + 1 < marks.shape[0]:
+        marks[...] = jnp.zeros(marks.shape, F32)
+    for line in range(last + 1):
+        for block in range(blocks):
+            marks[line : line + 1, block * wide : (block + 1) * wide] = jnp.full(
                 (1, wide), valid[0, line, block].astype(F32), F32
             )
+    tile[0, height:, :] = marks[...].astype(BF16)
     whole.wait()
+    tile[0, :height, :] = frames[0]
     spots = lax.broadcasted_iota(jnp.int32, (4, lanes), 0)
     tail = frames[0, height - 8 : height, :].astype(F32)[4:8]
     head = frames[0, 0:8, :].astype(F32)[0:4]
-    down = jnp.where(spots == 0, marks[0:1, :], tail)
-    upper = jnp.where(spots == 3, marks[3:4, :], head)
+    down = jnp.where(spots == 0, marks[last : last + 1, :], tail)
+    upper = jnp.where(spots == 3, marks[0:1, :], head)
     bands = {1: down, -1: upper}
     bands[0] = jnp.where(side("row", 1), down, upper)
     columns = {}
@@ -120,26 +123,19 @@
     )
 
 
-def prepare_kernel(held, sources, *refs):
-    far_refs, refs = refs[:6], refs[6:]
-    filter_outs, encoder_outs, refs = refs[:3], refs[3:6], refs[6:]
-    near_refs, (filter_staged, encoder_staged, sems) = refs[:6], refs[6:]
+def prepare_kernel(sources, *refs):
+    far_refs, refs = refs[:5], refs[5:]
+    filter_outs, encoder_outs, refs = refs[:2], refs[2:5], refs[5:]
+    near_refs, (filter_staged, encoder_staged, sems) = refs[:5], refs[5:]
     copies = fetch(*zip(far_refs, near_refs), sems)
     for copy in copies:
         copy.wait()
-    filter_matrix(held, *filter_outs, *near_refs[:3], filter_staged)
-    encoder_matrix(sources, *encoder_outs, *near_refs[3:], encoder_staged)
-
-
-def filter_matrix(held, out, shift, masks, weight, bias, valid, staged):
+    filter_matrix(*filter_outs, *near_refs[:2], filter_staged)
+    encoder_matrix(sources, *encoder_outs, *near_refs[2:], encoder_staged)
+
+
+def filter_matrix(out, shift, weight, bias, staged):
     shift[...] = jnp.broadcast_to(jnp.concatenate([bias[...]] * PX, axis=1), shift.shape)
-    spots = lax.broadcasted_iota(jnp.int32, (held, LANES), 0)
-    for c in range(valid.shape[2]):
-        mask = jnp.zeros((held, LANES), F32)
-        for line in range(valid.shape[1]):
-            inside = (spots >= 1 + 4 * line) & (spots < 5 + 4 * line)
-            mask = jnp.where(inside, valid[0, line, c].astype(F32), mask)
-        masks[c * held : (c + 1) * held, :] = mask
     tiled = turned(weight, staged)
     taps = {
         (dy, dx): tiled[(3 * dy + dx) * CH : (3 * dy + dx + 1) * CH]
@@ -209,11 +205,11 @@
 
 
 def pool_kernel(
-    order, stride, frames, up, dn, rt, lf, ur, ul, dr, dl, matrix, bias, masks, *refs
+    order, stride, crossed, tile, up, dn, rt, lf, ur, ul, dr, dl, matrix, bias, *refs
 ):
     outs, (x, pooled) = refs[:-2], refs[-2:]
-    height = frames.shape[1]
-    lanes = frames.shape[2]
+    height = rt.shape[0] // 2
+    lanes = tile.shape[2]
     groups = lanes // LANES
     blocks = groups // 2
     cells = groups // 2 + 1
@@ -221,8 +217,9 @@
     held = pooled.shape[0] // outs[0].shape[1]
     has_up = side("row", -1).astype(F32)
     has_dn = side("row", 1).astype(F32)
-    has_rt = side("col", 1).astype(F32)
-    has_lf = side("col", -1).astype(F32)
+    toward = -1 if crossed else 1
+    has_rt = side("col", toward).astype(F32)
+    has_lf = side("col", -toward).astype(F32)
     around = groups + 2
     pitch = x.shape[0] // around
     below = 8 + height
@@ -233,7 +230,7 @@
         base = g * pitch
         window = pl.ds(g * LANES, LANES)
         if g < groups:
-            own = frames[0, :, window].astype(F32)
+            own = tile[0, :height, window].astype(F32)
             over = up[:, window].astype(F32) * has_up
             under = dn[:, window].astype(F32) * has_dn
         elif g == groups:
@@ -281,8 +278,8 @@
             base = 2 * c * pitch
             above = x[base + 4 : base + 5, :]
             under = x[base + below + 3 : base + below + 4, :]
-            mask = masks[c * held : (c + 1) * held, :]
-            inside = []
+            marks = tile[0, height:, 2 * c * LANES : (2 * c + 1) * LANES].astype(F32)
+            inside = [marks[line : line + 1] for line in range(height // 8)]
         else:
             one = lax.broadcasted_iota(jnp.int32, (1, LANES), 1) < LANES // 2
 
@@ -401,34 +398,53 @@
     shaped = jax.ShapeDtypeStruct
     row_dirs, col_dirs = directions("row"), directions("col")
     n_col = lax.axis_size("col")
+    direct = bands <= 4
+    crossed = direct and n_col == 2
+    marked = up_to(height // 8, 8)
 
     band = shaped((4, lanes), BF16)
     column = shaped((2 * height, LANES), BF16)
     corner = shaped((4, LANES), BF16)
-    own, *sends = call(
+    tile, *sends = call(
         functools.partial(halo_kernel, row_dirs, col_dirs),
-        [shaped(frames.shape, BF16)]
+        [shaped((1, height + marked, lanes), BF16)]
         + [band] * len(row_dirs)
         + [column] * len(col_dirs)
         + [corner] * (len(row_dirs) * len(col_dirs)),
         [far(), far()],
-        [VMEM((8, lanes), F32), SMEM(valid_blocks.shape, jnp.int32), DMA((2,))],
+        [
+            VMEM(frames.shape, BF16),
+            VMEM((marked, lanes), F32),
+            SMEM(valid_blocks.shape, jnp.int32),
+            DMA((2,)),
+        ],
     )(in_far(frames), in_far(valid_blocks))
     sends = iter(sends)
-    by_row, by_col = {}, {}
+    by_row, by_col, by_both = {}, {}, {}
+    flip = [(0, 1), (1, 0)]
+
+    def product(first, second):
+        return [(a * n_col + c, b * n_col + d) for a, b in first for c, d in second]
+
     for w in row_dirs:
-        by_row[w] = lax.ppermute(next(sends), "row", pairs_of("row", w))
-    for w in col_dirs:
-        by_col[w] = lax.ppermute(next(sends), "col", pairs_of("col", w))
-    by_both = {}
+        if crossed:
+            pairs = product(pairs_of("row", w), flip)
+            by_row[w] = lax.ppermute(next(sends), ("row", "col"), pairs)
+        else:
+            by_row[w] = lax.ppermute(next(sends), "row", pairs_of("row", w))
+    for v in col_dirs:
+        if crossed:
+            by_col[v] = next(sends)
+            tile = lax.ppermute(tile, "col", flip)
+        else:
+            by_col[v] = lax.ppermute(next(sends), "col", pairs_of("col", v))
     for w in row_dirs:
         for v in col_dirs:
-            pairs = [
-                (a * n_col + c, b * n_col + d)
-                for a, b in pairs_of("row", w)
-                for c, d in pairs_of("col", v)
-            ]
-            by_both[w, v] = lax.ppermute(next(sends), ("row", "col"), pairs)
+            if crossed:
+                by_both[w, v] = lax.ppermute(next(sends), "row", pairs_of("row", w))
+            else:
+                pairs = product(pairs_of("row", w), pairs_of("col", v))
+                by_both[w, v] = lax.ppermute(next(sends), ("row", "col"), pairs)
 
     def pick(table, way):
         return table[way] if way in table else table[0]
@@ -442,7 +458,6 @@
     held = up_to(rows + 2, 8)
     kept = up_to(cells, 8)
     piece = shaped((stride + 2, kept, LANES), BF16)
-    direct = bands <= 4
     if direct:
         order = [functools.partial(lambda k, me: lax.rem(me + k, bands), k) for k in range(bands)]
         sources = [
@@ -452,48 +467,45 @@
     else:
         order = [functools.partial(lambda k, me: k, k) for k in range(bands)]
         sources = order
-    filter_table, filter_shift, masks, encoder_table, encoder_shift, picks = call(
-        functools.partial(prepare_kernel, held, sources),
+    filter_table, filter_shift, encoder_table, encoder_shift, picks = call(
+        functools.partial(prepare_kernel, sources),
         [
             shaped((12 * LANES, 2 * LANES), BF16),
             shaped((8, LANES), F32),
-            shaped(((cells - 1) * held, LANES), F32),
             shaped((6 * LANES, 3 * PX * OUTC), BF16),
             shaped((8, PX * OUTC), F32),
             shaped((bands, kept, LANES), jnp.int32),
         ],
-        [far()] * 6,
+        [far()] * 5,
         [
             VMEM((CH, 9 * CH), BF16),
             VMEM((1, CH), F32),
-            SMEM(valid_blocks.shape, jnp.int32),
             VMEM((OUTC, 27 * CH), BF16),
             VMEM((1, OUTC), F32),
             SMEM(owner_map.shape, jnp.int32),
             VMEM((LANES, up_to(9 * CH, LANES)), F32),
             VMEM((LANES, up_to(27 * CH, LANES)), F32),
-            DMA((6,)),
+            DMA((5,)),
         ],
         (1 << 22, 1 << 20),
     )(
         in_far(deblock_weight.T),
         in_far(deblock_bias.reshape(1, CH)),
-        in_far(valid_blocks),
         in_far(encoder_weight.T),
         in_far(encoder_bias.reshape(1, OUTC)),
         in_far(owner_map),
     )
     parts = call(
-        functools.partial(pool_kernel, order, stride),
+        functools.partial(pool_kernel, order, stride, crossed),
         [piece] * bands,
-        [vm()] * 12,
+        [vm()] * 11,
         [
             VMEM(((lanes // LANES + 2) * up_to(8 + 2 * held, 8), LANES), F32),
             VMEM((kept * held, LANES), F32),
         ],
         (1 << 22, 1 << 20),
     )(
-        own,
+        tile,
         pick(by_row, 1),
         pick(by_row, -1),
         pick(by_col, -1),
@@ -504,13 +516,18 @@
         pick_both(-1, 1),
         filter_table,
         filter_shift,
-        masks,
     )
     if direct:
-        arrived = [parts[0]]
-        for k in range(1, bands):
-            pairs = [(i, (i + k) % bands) for i in range(bands)]
-            arrived.append(lax.ppermute(parts[k], "tm", pairs))
+        arrived = []
+        for k in range(bands):
+            shift = [(i, (i + k) % bands) for i in range(bands)]
+            if crossed:
+                pairs = product(shift, flip)
+                arrived.append(lax.ppermute(parts[k], ("tm", "col"), pairs))
+            elif k:
+                arrived.append(lax.ppermute(parts[k], "tm", shift))
+            else:
+                arrived.append(parts[k])
     else:
         arrived = [
             lax.all_to_all(jnp.stack(parts), "tm", split_axis=0, concat_axis=0, tiled=True)

time: 16.5 us -> 16.4 us (level)
  starting transfers between devices: 8.79 us -> 8.6 us
    ppermute x6 -> x7, starting transfers between devices: 8.79 us -> 8.6 us  [the longest x4 5.41 us: on_device(): arrived.append(lax.ppermute(parts[k], ('tm', 'col'), pairs))]
    ppermute x6 -> x7, waiting for transfers between devices: 3.85 us -> 3.96 us  [the longest x1 2.16 us: on_device(): by_both[w, v] = lax.ppermute(next(sends), 'row', pairs_of('row', w))]
  transfers between devices with their start and end apart: 6 -> 7, of which waited for: 4 -> 3; matrix products, arithmetic and copies ran while one was open for 0% -> 0% of each run, Pallas kernels for 8% -> 8%
where the time goes in v4:
time: 16.4 us; the launch traced here: 16.2 us
  starting transfers between devices  8.6 us (52%)
  waiting for transfers between devices  3.96 us (24%)
  Pallas kernels  3.62 us (22%)
    ppermute x4, starting transfers between devices, on_device(): arrived.append(lax.ppermute(parts[k], ('tm', 'col'), pairs))  5.41 us
    ppermute x1, starting transfers between devices, on_device(): by_row[w] = lax.ppermute(next(sends), ('row', 'col'), pairs)  2.59 us
    ppermute x1, waiting for transfers between devices, on_device(): by_both[w, v] = lax.ppermute(next(sends), 'row', pairs_of('row', w))  2.16 us
    ppermute x4, waiting for transfers between devices, on_device(): arrived.append(lax.ppermute(parts[k], ('tm', 'col'), pairs))  1.79 us
    pallas_call x1, Pallas kernels, on_device(): call(functools.partial(prepare_kernel, sources), [shaped((12 * LANES, 2 *...  1.36 us
    pallas_call x1, Pallas kernels, on_device(): call(encode_kernel, shaped((1, stride, bands - 1, lanes // 2 // CH * OUTC...  0.96 us
    pallas_call x1, Pallas kernels, on_device(): call(functools.partial(halo_kernel, row_dirs, col_dirs), [shaped((1, heig...  0.94 us
    ppermute x1, starting transfers between devices, on_device(): tile = lax.ppermute(tile, 'col', flip)  0.56 us
  transfers between devices with their start and end apart: 7, of which 3 were waited for; matrix products, arithmetic and copies ran while one was open for 0% of the time, Pallas kernels for 8%

profile of v4, /device:TPU:0, one launch (start us, length us, event | category | flops | bytes accessed | tf_op | source)
XLA Modules:
  0.0 16.2 jit_solution(182216645612011742)
XLA Ops:
  0.0 0.9 %shard_map.74 = (bf16[1,16,4608]{2,1,0:T(8,128)(2,1)S(1)}, bf16[4,4608]{1,0:T(4,128)(2,1)S(1)}, bf16[16,128]{1,0:T(8,128)(2,1)S(1)}, bf16[4,128]{1,0:T(4,128)(2,1)S(1)}) custom-call(bf16[1,8,4608]{2,1,0:T(8,128)(2,1)} %frames_far.1, s32[1,1,18]{2,1,0:T(1,128)} %valid_far.1), custom_call_target="tpu_custom_call" | custom-call | tf_op jit(solution)/shard_map/pallas_call | solution.py:408
  0.9 0.6 %collective-permute-start = (bf16[1,16,4608]{2,1,0:T(8,128)(2,1)S(1)}, bf16[1,16,4608]{2,1,0:T(8,128)(2,1)S(1)}, u32[]{:S(2)}, u32[]{:S(2)}) collective-permute-start(bf16[1,16,4608]{2,1,0:T(8,128)(2,1)S(1)} %get-tuple-element.21), channel_id=1, source_target_pairs={{0,1},{1,0},{2,3},{3,2},{4,5},{5,4},{6,7},{7,6},{8,9},{9,8},{10,11... | collective-permute-start | bytes 442376 | tf_op jit(solution)/shard_map/ppermute | solution.py:438
  1.5 2.6 %collective-permute-start.1 = (bf16[4,4608]{1,0:T(4,128)(2,1)S(1)}, bf16[4,4608]{1,0:T(4,128)(2,1)S(1)}, u32[]{:S(2)}, u32[]{:S(2)}) collective-permute-start(bf16[4,4608]{1,0:T(4,128)(2,1)S(1)} %get-tuple-element.22), channel_id=1, source_target_pairs={{0,3},{1,2},{2,1},{3,0},{4,7},{5,6},{6,5},{7,4},{8,11},{9,10},{10,... | collective-permute-start | bytes 110600 | tf_op jit(solution)/shard_map/ppermute | solution.py:432
  4.1 0.0 collective-permute-start.2
  4.1 1.4 %shard_map.73 = (bf16[1536,256]{1,0:T(8,128)(2,1)S(1)}, f32[8,128]{1,0:T(8,128)S(1)}, bf16[768,768]{1,0:T(8,128)(2,1)S(1)}, f32[8,256]{1,0:T(8,128)S(1)}, s32[4,24,128]{2,1,0:T(8,128)S(1)}) custom-call(bf16[32,288]{1,0:T(8,128)(2,1)} %bitcast.6, f32[1,32]{1,0:T(1,128)} %bitcast.7, bf16[64,864]{1,0:T(8,128)(2,1)} %bitcast.5, f32[1,64]{1,0:T(1,128)} %bitcast.8, ...), custom_call_target="tpu_custom_call" | custom-call | flops 4194304 | bytes 1048576 | tf_op jit(solution)/shard_map/pallas_call | solution.py:470
  5.5 2.2 %collective-permute-done.2.ur.ul.dr.dl = bf16[4,128]{1,0:T(4,128)(2,1)S(1)} collective-permute-done((bf16[4,128]{1,0:T(4,128)(2,1)S(1)}, bf16[4,128]{1,0:T(4,128)(2,1)S(1)}, u32[]{:S(2)}, u32[]{:S(2)}) %collective-permute-start.2) | collective-permute-done | bytes 1056 | tf_op jit(solution)/shard_map/ppermute | solution.py:444
  7.7 0.0 collective-permute-done.1.up.dn
  7.7 0.0 collective-permute-done.tile
  7.7 0.4 %shard_map.75 = (bf16[3,24,128]{2,1,0:T(8,128)(2,1)S(1)}, bf16[3,24,128]{2,1,0:T(8,128)(2,1)S(1)}, bf16[3,24,128]{2,1,0:T(8,128)(2,1)S(1)}, bf16[3,24,128]{2,1,0:T(8,128)(2,1)S(1)}) custom-call(bf16[1,16,4608]{2,1,0:T(8,128)(2,1)S(1)} %collective-permute-done.tile, bf16[4,4608]{1,0:T(4,128)(2,1)S(1)} %collective-permute-done.1.up.dn, ...), custom_call_target="tpu_custom_call" | custom-call | flops 4194304 | bytes 1048576 | tf_op jit(solution)/shard_map/pallas_call | solution.py:498
  8.0 0.1 collective-permute-start.3
  8.1 1.7 %collective-permute-start.4 = (bf16[3,24,128]{2,1,0:T(8,128)(2,1)S(1)}, bf16[3,24,128]{2,1,0:T(8,128)(2,1)S(1)}, u32[]{:S(2)}, u32[]{:S(2)}) collective-permute-start(bf16[3,24,128]{2,1,0:T(8,128)(2,1)S(1)} %get-tuple-element.28), channel_id=1, source_target_pairs={{0,5},{1,4},{4,9},{5,8},{8,13},{9,12},{12,1},{13,0},{2,7},{3,6},{6... | collective-permute-start | bytes 55304 | tf_op jit(solution)/shard_map/ppermute | solution.py:526
  9.8 2.3 %collective-permute-start.5 = (bf16[3,24,128]{2,1,0:T(8,128)(2,1)S(1)}, bf16[3,24,128]{2,1,0:T(8,128)(2,1)S(1)}, u32[]{:S(2)}, u32[]{:S(2)}) collective-permute-start(bf16[3,24,128]{2,1,0:T(8,128)(2,1)S(1)} %get-tuple-element.29), channel_id=1, source_target_pairs={{0,9},{1,8},{4,13},{5,12},{8,1},{9,0},{12,5},{13,4},{2,11},{3,10},... | collective-permute-start | bytes 55304 | tf_op jit(solution)/shard_map/ppermute | solution.py:526
  12.1 1.4 %collective-permute-start.6 = (bf16[3,24,128]{2,1,0:T(8,128)(2,1)S(1)}, bf16[3,24,128]{2,1,0:T(8,128)(2,1)S(1)}, u32[]{:S(2)}, u32[]{:S(2)}) collective-permute-start(bf16[3,24,128]{2,1,0:T(8,128)(2,1)S(1)} %get-tuple-element.30), channel_id=1, source_target_pairs={{0,13},{1,12},{4,1},{5,0},{8,5},{9,4},{12,9},{13,8},{2,15},{3,14},... | collective-permute-start | bytes 55304 | tf_op jit(solution)/shard_map/ppermute | solution.py:526
  13.5 0.0 collective-permute-done.3.refs_0_
  13.5 0.0 collective-permute-done.4.refs_1_
  13.5 0.6 %collective-permute-done.5.refs_2_ = bf16[3,24,128]{2,1,0:T(8,128)(2,1)S(1)} collective-permute-done((bf16[3,24,128]{2,1,0:T(8,128)(2,1)S(1)}, bf16[3,24,128]{2,1,0:T(8,128)(2,1)S(1)}, u32[]{:S(2)}, u32[]{:S(2)}) %collective-permute-start.5) | collective-permute-done | bytes 18464 | tf_op jit(solution)/shard_map/ppermute | solution.py:526
  14.0 1.2 %collective-permute-done.6.refs_3_ = bf16[3,24,128]{2,1,0:T(8,128)(2,1)S(1)} collective-permute-done((bf16[3,24,128]{2,1,0:T(8,128)(2,1)S(1)}, bf16[3,24,128]{2,1,0:T(8,128)(2,1)S(1)}, u32[]{:S(2)}, u32[]{:S(2)}) %collective-permute-start.6) | collective-permute-done | bytes 18464 | tf_op jit(solution)/shard_map/ppermute | solution.py:526
  15.2 1.0 %shard_map.76 = bf16[1,1,3,4608]{3,2,1,0:T(4,128)(2,1)} custom-call(bf16[768,768]{1,0:T(8,128)(2,1)S(1)} %get-tuple-element.18.matrix, f32[8,256]{1,0:T(8,128)S(1)} %get-tuple-element.19.bias, s32[4,24,128]{2,1,0:T(8,128)S(1)} %get-tuple-element.20.picks, bf16[3,24,128]{2,1,0:T(8,128)(2,1)S(1)} %collective-permute-done.3.refs_0_, ...), custom_call_target="tpu_custom_call" | custom-call | flops 4194304 | bytes 1048576 | tf_op jit(solution)/shard_map/pallas_call | solution.py:535
Async XLA Ops:
  0.9 6.7 %collective-permute-start = (bf16[1,16,4608]{2,1,0:T(8,128)(2,1)S(1)}, bf16[1,16,4608]{2,1,0:T(8,128)(2,1)S(1)}, u32[]{:S(2)}, u32[]{:S(2)}) collective-permute-start(bf16[1,16,4608]{2,1,0:T(8,128)(2,1)S(1)} %get-tuple-element.21), channel_id=1, source_target_pairs={{0,1},{1,0},{2,3},{3,2},{4,5},{5,4},{6,7},{7,6},{8,9},{9,8},{10,11... | collective-permute-start | bytes 442376 | tf_op jit(solution)/shard_map/ppermute | solution.py:438
  1.5 6.2 %collective-permute-start.1 = (bf16[4,4608]{1,0:T(4,128)(2,1)S(1)}, bf16[4,4608]{1,0:T(4,128)(2,1)S(1)}, u32[]{:S(2)}, u32[]{:S(2)}) collective-permute-start(bf16[4,4608]{1,0:T(4,128)(2,1)S(1)} %get-tuple-element.22), channel_id=1, source_target_pairs={{0,3},{1,2},{2,1},{3,0},{4,7},{5,6},{6,5},{7,4},{8,11},{9,10},{10,... | collective-permute-start | bytes 110600 | tf_op jit(solution)/shard_map/ppermute | solution.py:432
  4.1 3.6 %collective-permute-start.2 = (bf16[4,128]{1,0:T(4,128)(2,1)S(1)}, bf16[4,128]{1,0:T(4,128)(2,1)S(1)}, u32[]{:S(2)}, u32[]{:S(2)}) collective-permute-start(bf16[4,128]{1,0:T(4,128)(2,1)S(1)} %get-tuple-element.24), channel_id=1, source_target_pairs={{0,2},{2,0},{1,3},{3,1},{4,6},{6,4},{5,7},{7,5},{8,10},{10,8},{9,1... | collective-permute-start | bytes 3080 | tf_op jit(solution)/shard_map/ppermute | solution.py:444
  8.0 5.4 %collective-permute-start.3 = (bf16[3,24,128]{2,1,0:T(8,128)(2,1)S(1)}, bf16[3,24,128]{2,1,0:T(8,128)(2,1)S(1)}, u32[]{:S(2)}, u32[]{:S(2)}) collective-permute-start(bf16[3,24,128]{2,1,0:T(8,128)(2,1)S(1)} %get-tuple-element.27), channel_id=1, source_target_pairs={{0,1},{1,0},{4,5},{5,4},{8,9},{9,8},{12,13},{13,12},{2,3},{3,2},{6... | collective-permute-start | bytes 55304 | tf_op jit(solution)/shard_map/ppermute | solution.py:526
  8.1 5.3 %collective-permute-start.4 = (bf16[3,24,128]{2,1,0:T(8,128)(2,1)S(1)}, bf16[3,24,128]{2,1,0:T(8,128)(2,1)S(1)}, u32[]{:S(2)}, u32[]{:S(2)}) collective-permute-start(bf16[3,24,128]{2,1,0:T(8,128)(2,1)S(1)} %get-tuple-element.28), channel_id=1, source_target_pairs={{0,5},{1,4},{4,9},{5,8},{8,13},{9,12},{12,1},{13,0},{2,7},{3,6},{6... | collective-permute-start | bytes 55304 | tf_op jit(solution)/shard_map/ppermute | solution.py:526
  9.8 4.2 %collective-permute-start.5 = (bf16[3,24,128]{2,1,0:T(8,128)(2,1)S(1)}, bf16[3,24,128]{2,1,0:T(8,128)(2,1)S(1)}, u32[]{:S(2)}, u32[]{:S(2)}) collective-permute-start(bf16[3,24,128]{2,1,0:T(8,128)(2,1)S(1)} %get-tuple-element.29), channel_id=1, source_target_pairs={{0,9},{1,8},{4,13},{5,12},{8,1},{9,0},{12,5},{13,4},{2,11},{3,10},... | collective-permute-start | bytes 55304 | tf_op jit(solution)/shard_map/ppermute | solution.py:526
  12.1 3.2 %collective-permute-start.6 = (bf16[3,24,128]{2,1,0:T(8,128)(2,1)S(1)}, bf16[3,24,128]{2,1,0:T(8,128)(2,1)S(1)}, u32[]{:S(2)}, u32[]{:S(2)}) collective-permute-start(bf16[3,24,128]{2,1,0:T(8,128)(2,1)S(1)} %get-tuple-element.30), channel_id=1, source_target_pairs={{0,13},{1,12},{4,1},{5,0},{8,5},{9,4},{12,9},{13,8},{2,15},{3,14},... | collective-permute-start | bytes 55304 | tf_op jit(solution)/shard_map/ppermute | solution.py:526

commit v5 on v3

--- a/solution.py
+++ b/solution.py
@@ -56,8 +56,8 @@
     return (0,) if lax.axis_size(axis) <= 2 else (1, -1)
 
 
-def halo_kernel(row_dirs, col_dirs, frames_far, valid_far, frames, *refs):
-    sends, (marks, valid, sems) = refs[:-3], refs[-3:]
+def halo_kernel(row_dirs, col_dirs, crossed, frames_far, valid_far, *refs):
+    sends, (frames, marks, valid, sems) = refs[:-4], refs[-4:]
     whole, flags = fetch((frames_far, frames), (valid_far, valid), sems)
     flags.wait()
     height = frames.shape[1]
@@ -96,7 +96,7 @@
         next(outs)[...] = bands[way].astype(BF16)
     for way in col_dirs:
         next(outs)[...] = columns[way].astype(BF16)
-    for row_way in row_dirs:
+    for row_way in () if crossed else row_dirs:
         for col_way in col_dirs:
             right = bands[row_way][:, lanes - LANES :]
             left = bands[row_way][:, :LANES]
@@ -105,6 +105,35 @@
             else:
                 picked = right if col_way > 0 else left
             next(outs)[...] = picked.astype(BF16)
+
+
+def corner_kernel(row_dirs, frames, valid, *refs):
+    count = len(row_dirs)
+    bands, outs = refs[:count], refs[count:]
+    height = frames.shape[1]
+    lanes = frames.shape[2]
+    first = side("col", 1)
+    flags = valid[0].astype(F32)
+    blocks = flags.shape[1]
+    lane = lax.broadcasted_iota(jnp.int32, (1, blocks), 1)
+    wanted = jnp.where(first, 0, blocks - 1)
+
+    def mark(line):
+        row = jnp.where(lane == wanted, flags[line : line + 1], 0.0)
+        return jnp.broadcast_to(jnp.sum(row, axis=1, keepdims=True), (4, LANES))
+
+    def edge(start):
+        left = frames[0, start : start + 8, :LANES].astype(F32)
+        right = frames[0, start : start + 8, lanes - LANES :].astype(F32)
+        return jnp.where(first, left, right)
+
+    spots = lax.broadcasted_iota(jnp.int32, (4, LANES), 0)
+    down = jnp.where(spots == 0, mark(flags.shape[0] - 1), edge(height - 8)[4:8])
+    upper = jnp.where(spots == 3, mark(0), edge(0)[0:4])
+    corners = {1: down, -1: upper, 0: jnp.where(side("row", 1), down, upper)}
+    for way, band, out in zip(row_dirs, bands, outs):
+        out[:, :lanes] = band[...]
+        out[:, lanes:] = corners[way].astype(BF16)
 
 
 def turned(weight, staged):
@@ -209,11 +238,13 @@
 
 
 def pool_kernel(
-    order, stride, frames, up, dn, rt, lf, ur, ul, dr, dl, matrix, bias, masks, *refs
+    order, stride, crossed, tile, matrix, bias, masks, up, dn, rt, lf, *refs
 ):
+    if not crossed:
+        (ur, ul, dr, dl), refs = refs[:4], refs[4:]
     outs, (x, pooled) = refs[:-2], refs[-2:]
-    height = frames.shape[1]
-    lanes = frames.shape[2]
+    height = rt.shape[0] // 2
+    lanes = tile.shape[2]
     groups = lanes // LANES
     blocks = groups // 2
     cells = groups // 2 + 1
@@ -221,8 +252,12 @@
     held = pooled.shape[0] // outs[0].shape[1]
     has_up = side("row", -1).astype(F32)
     has_dn = side("row", 1).astype(F32)
-    has_rt = side("col", 1).astype(F32)
-    has_lf = side("col", -1).astype(F32)
+    if crossed:
+        ur = ul = up.at[:, lanes : lanes + LANES]
+        dr = dl = dn.at[:, lanes : lanes + LANES]
+    toward = -1 if crossed else 1
+    has_rt = side("col", toward).astype(F32)
+    has_lf = side("col", -toward).astype(F32)
     around = groups + 2
     pitch = x.shape[0] // around
     below = 8 + height
@@ -233,7 +268,7 @@
         base = g * pitch
         window = pl.ds(g * LANES, LANES)
         if g < groups:
-            own = frames[0, :, window].astype(F32)
+            own = tile[0, :height, window].astype(F32)
             over = up[:, window].astype(F32) * has_up
             under = dn[:, window].astype(F32) * has_dn
         elif g == groups:
@@ -401,34 +436,56 @@
     shaped = jax.ShapeDtypeStruct
     row_dirs, col_dirs = directions("row"), directions("col")
     n_col = lax.axis_size("col")
+    direct = bands <= 4
+    crossed = direct and n_col == 2
 
     band = shaped((4, lanes), BF16)
     column = shaped((2 * height, LANES), BF16)
     corner = shaped((4, LANES), BF16)
-    own, *sends = call(
-        functools.partial(halo_kernel, row_dirs, col_dirs),
-        [shaped(frames.shape, BF16)]
-        + [band] * len(row_dirs)
+    tile, flags = frames, in_far(valid_blocks)
+    flip = [(0, 1), (1, 0)]
+
+    def product(first, second):
+        return [(a * n_col + c, b * n_col + d) for a, b in first for c, d in second]
+
+    if crossed:
+        tile = lax.ppermute(frames, "col", flip)
+        flags = lax.ppermute(valid_blocks, "col", flip)
+    sends = call(
+        functools.partial(halo_kernel, row_dirs, col_dirs, crossed),
+        [band] * len(row_dirs)
         + [column] * len(col_dirs)
-        + [corner] * (len(row_dirs) * len(col_dirs)),
+        + [corner] * (0 if crossed else len(row_dirs) * len(col_dirs)),
         [far(), far()],
-        [VMEM((8, lanes), F32), SMEM(valid_blocks.shape, jnp.int32), DMA((2,))],
+        [
+            VMEM(frames.shape, BF16),
+            VMEM((8, lanes), F32),
+            SMEM(valid_blocks.shape, jnp.int32),
+            DMA((2,)),
+        ],
     )(in_far(frames), in_far(valid_blocks))
-    sends = iter(sends)
-    by_row, by_col = {}, {}
-    for w in row_dirs:
-        by_row[w] = lax.ppermute(next(sends), "row", pairs_of("row", w))
-    for w in col_dirs:
-        by_col[w] = lax.ppermute(next(sends), "col", pairs_of("col", w))
-    by_both = {}
-    for w in row_dirs:
-        for v in col_dirs:
-            pairs = [
-                (a * n_col + c, b * n_col + d)
-                for a, b in pairs_of("row", w)
-                for c, d in pairs_of("col", v)
-            ]
-            by_both[w, v] = lax.ppermute(next(sends), ("row", "col"), pairs)
+    row_sends, sends = sends[: len(row_dirs)], iter(sends[len(row_dirs) :])
+    if crossed:
+        row_sends = call(
+            functools.partial(corner_kernel, row_dirs),
+            [shaped((4, lanes + LANES), BF16)] * len(row_dirs),
+            [vm()] * (2 + len(row_dirs)),
+            [],
+        )(tile, flags, *row_sends)
+    by_row, by_col, by_both = {}, {}, {}
+    for w, send in zip(row_dirs, row_sends):
+        if crossed:
+            pairs = product(pairs_of("row", w), flip)
+            by_row[w] = lax.ppermute(send, ("row", "col"), pairs)
+        else:
+            by_row[w] = lax.ppermute(send, "row", pairs_of("row", w))
+    for v in col_dirs:
+        by_col[v] = next(sends)
+        if not crossed:
+            by_col[v] = lax.ppermute(by_col[v], "col", pairs_of("col", v))
+    for w, v in () if crossed else [(w, v) for w in row_dirs for v in col_dirs]:
+        pairs = product(pairs_of("row", w), pairs_of("col", v))
+        by_both[w, v] = lax.ppermute(next(sends), ("row", "col"), pairs)
 
     def pick(table, way):
         return table[way] if way in table else table[0]
@@ -442,7 +499,6 @@
     held = up_to(rows + 2, 8)
     kept = up_to(cells, 8)
     piece = shaped((stride + 2, kept, LANES), BF16)
-    direct = bands <= 4
     if direct:
         order = [functools.partial(lambda k, me: lax.rem(me + k, bands), k) for k in range(bands)]
         sources = [
@@ -462,7 +518,7 @@
             shaped((8, PX * OUTC), F32),
             shaped((bands, kept, LANES), jnp.int32),
         ],
-        [far()] * 6,
+        [far(), far(), vm() if crossed else far(), far(), far(), far()],
         [
             VMEM((CH, 9 * CH), BF16),
             VMEM((1, CH), F32),
@@ -478,39 +534,35 @@
     )(
         in_far(deblock_weight.T),
         in_far(deblock_bias.reshape(1, CH)),
-        in_far(valid_blocks),
+        flags,
         in_far(encoder_weight.T),
         in_far(encoder_bias.reshape(1, OUTC)),
         in_far(owner_map),
     )
+    around = [pick(by_row, 1), pick(by_row, -1), pick(by_col, -1), pick(by_col, 1)]
+    if not crossed:
+        around += [pick_both(w, v) for w in (1, -1) for v in (-1, 1)]
     parts = call(
-        functools.partial(pool_kernel, order, stride),
+        functools.partial(pool_kernel, order, stride, crossed),
         [piece] * bands,
-        [vm()] * 12,
+        [vm()] * (4 + len(around)),
         [
             VMEM(((lanes // LANES + 2) * up_to(8 + 2 * held, 8), LANES), F32),
             VMEM((kept * held, LANES), F32),
         ],
         (1 << 22, 1 << 20),
-    )(
-        own,
-        pick(by_row, 1),
-        pick(by_row, -1),
-        pick(by_col, -1),
-        pick(by_col, 1),
-        pick_both(1, -1),
-        pick_both(1, 1),
-        pick_both(-1, -1),
-        pick_both(-1, 1),
-        filter_table,
-        filter_shift,
-        masks,
-    )
+    )(tile, filter_table, filter_shift, masks, *around)
     if direct:
-        arrived = [parts[0]]
-        for k in range(1, bands):
-            pairs = [(i, (i + k) % bands) for i in range(bands)]
-            arrived.append(lax.ppermute(parts[k], "tm", pairs))
+        arrived = []
+        for k in range(bands):
+            shift = [(i, (i + k) % bands) for i in range(bands)]
+            if crossed:
+                pairs = product(shift, flip)
+                arrived.append(lax.ppermute(parts[k], ("tm", "col"), pairs))
+            elif k:
+                arrived.append(lax.ppermute(parts[k], "tm", shift))
+            else:
+                arrived.append(parts[k])
     else:
         arrived = [
             lax.all_to_all(jnp.stack(parts), "tm", split_axis=0, concat_axis=0, tiled=True)

time: 16.5 us -> 15.4 us (0.933)
  waiting for transfers between devices: 3.85 us -> 2.68 us
    ppermute x6 -> x7, waiting for transfers between devices: 3.85 us -> 2.68 us  [the longest x4 2.04 us: on_device(): arrived.append(lax.ppermute(parts[k], ('tm', 'col'), pairs))]
    pallas_call x2 -> x3, Pallas kernels: 1.3 us -> 1.38 us  [the longest x1 0.94 us: on_device(): call(functools.partial(halo_kernel, row_dirs, col_dirs, crossed), [band]...]
    ppermute x6 -> x7, starting transfers between devices: 8.79 us -> 8.81 us  [the longest x4 5.71 us: on_device(): arrived.append(lax.ppermute(parts[k], ('tm', 'col'), pairs))]
  transfers between devices with their start and end apart: 6 -> 7, of which waited for: 4 -> 4; matrix products, arithmetic and copies ran while one was open for 0% -> 0% of each run, Pallas kernels for 8% -> 15%
where the time goes in v5:
time: 15.4 us; the launch traced here: 15.2 us
  starting transfers between devices  8.81 us (57%)
  Pallas kernels  3.71 us (24%)
  waiting for transfers between devices  2.68 us (17%)
    ppermute x4, starting transfers between devices, on_device(): arrived.append(lax.ppermute(parts[k], ('tm', 'col'), pairs))  5.71 us
    ppermute x1, starting transfers between devices, on_device(): by_row[w] = lax.ppermute(send, ('row', 'col'), pairs)  2.59 us
    ppermute x4, waiting for transfers between devices, on_device(): arrived.append(lax.ppermute(parts[k], ('tm', 'col'), pairs))  2.04 us
    pallas_call x1, Pallas kernels, on_device(): call(functools.partial(prepare_kernel, held, sources), [shaped((12 * LANE...  1.37 us
    pallas_call x1, Pallas kernels, on_device(): call(encode_kernel, shaped((1, stride, bands - 1, lanes // 2 // CH * OUTC...  0.96 us
    pallas_call x1, Pallas kernels, on_device(): call(functools.partial(halo_kernel, row_dirs, col_dirs, crossed), [band]...  0.94 us
    ppermute x1, starting transfers between devices, on_device(): tile = lax.ppermute(frames, 'col', flip)  0.49 us
    pallas_call x1, Pallas kernels, on_device(): call(functools.partial(pool_kernel, order, stride, crossed), [piece] * ba...  0.35 us
  transfers between devices with their start and end apart: 7, of which 4 were waited for; matrix products, arithmetic and copies ran while one was open for 0% of the time, Pallas kernels for 15%

profile of v5, /device:TPU:0, one launch (start us, length us, event | category | flops | bytes accessed | tf_op | source)
XLA Modules:
  0.0 15.2 jit_solution(7469772273002899213)
XLA Ops:
  0.0 0.5 %collective-permute-start.1 = (bf16[1,8,4608]{2,1,0:T(8,128)(2,1)}, bf16[1,8,4608]{2,1,0:T(8,128)(2,1)S(1)}, u32[]{:S(2)}, u32[]{:S(2)}) collective-permute-start(bf16[1,8,4608]{2,1,0:T(8,128)(2,1)} %frames_far.1), channel_id=1, source_target_pairs={{0,1},{1,0},{2,3},{3,2},{4,5},{5,4},{6,7},{7,6},{8,9},{9,8},{10,11... | collective-permute-start | bytes 221192 | tf_op jit(solution)/shard_map/ppermute | solution.py:452
  0.5 0.0 collective-permute-start
  0.5 0.9 %shard_map.74 = (bf16[4,4608]{1,0:T(4,128)(2,1)S(1)}, bf16[16,128]{1,0:T(8,128)(2,1)S(1)}) custom-call(bf16[1,8,4608]{2,1,0:T(8,128)(2,1)} %frames_far.1, s32[1,1,18]{2,1,0:T(1,128)} %valid_far.1), custom_call_target="tpu_custom_call" | custom-call | tf_op jit(solution)/shard_map/pallas_call | solution.py:454
  1.5 0.3 %collective-permute-done.refs_2_.valid = s32[1,1,18]{2,1,0:T(1,128)S(1)} collective-permute-done((s32[1,1,18]{2,1,0:T(1,128)}, s32[1,1,18]{2,1,0:T(1,128)S(1)}, u32[]{:S(2)}, u32[]{:S(2)}) %collective-permute-start) | collective-permute-done | bytes 104 | tf_op jit(solution)/shard_map/ppermute | solution.py:453
  1.8 0.0 collective-permute-done.1.frames.tile
  1.8 0.1 shard_map.75
  1.9 2.6 %collective-permute-start.2 = (bf16[4,4736]{1,0:T(4,128)(2,1)S(1)}, bf16[4,4736]{1,0:T(4,128)(2,1)S(1)}, u32[]{:S(2)}, u32[]{:S(2)}) collective-permute-start(bf16[4,4736]{1,0:T(4,128)(2,1)S(1)} %shard_map.75), channel_id=1, source_target_pairs={{0,3},{1,2},{2,1},{3,0},{4,7},{5,6},{6,5},{7,4},{8,11},{9,10},{10,... | collective-permute-start | bytes 113672 | tf_op jit(solution)/shard_map/ppermute | solution.py:479
  4.5 1.4 %shard_map.73 = (bf16[1536,256]{1,0:T(8,128)(2,1)S(1)}, f32[8,128]{1,0:T(8,128)S(1)}, f32[144,128]{1,0:T(8,128)S(1)}, bf16[768,768]{1,0:T(8,128)(2,1)S(1)}, f32[...) custom-call(bf16[32,288]{1,0:T(8,128)(2,1)} %bitcast.6, f32[1,32]{1,0:T(1,128)} %bitcast.7, ...), custom_call_target="tpu_custom_call" | custom-call | flops 4194304 | bytes 1048576 | tf_op jit(solution)/shard_map/pallas_call | solution.py:511
  5.8 0.3 %collective-permute-done.2.up.dn = bf16[4,4736]{1,0:T(4,128)(2,1)S(1)} collective-permute-done((bf16[4,4736]{1,0:T(4,128)(2,1)S(1)}, bf16[4,4736]{1,0:T(4,128)(2,1)S(1)}, u32[]{:S(2)}, u32[]{:S(2)}) %collective-permute-start.2) | collective-permute-done | bytes 37920 | tf_op jit(solution)/shard_map/ppermute | solution.py:479
  6.2 0.4 %shard_map.76 = (bf16[3,24,128]{2,1,0:T(8,128)(2,1)S(1)}, bf16[3,24,128]{2,1,0:T(8,128)(2,1)S(1)}, bf16[3,24,128]{2,1,0:T(8,128)(2,1)S(1)}, bf16[3,24,128]{2,1,0:T(8,128)(2,1)S(1)}) custom-call(bf16[1,8,4608]{2,1,0:T(8,128)(2,1)S(1)} %collective-permute-done.1.frames.tile, bf16[1536,256]{1,0:T(8,128)(2,1)S(1)} %get-tuple-element.20.matrix, ...), custom_call_target="tpu_custom_call" | custom-call | flops 4194304 | bytes 1048576 | tf_op jit(solution)/shard_map/pallas_call | solution.py:545
  6.5 0.3 %collective-permute-start.3 = (bf16[3,24,128]{2,1,0:T(8,128)(2,1)S(1)}, bf16[3,24,128]{2,1,0:T(8,128)(2,1)S(1)}, u32[]{:S(2)}, u32[]{:S(2)}) collective-permute-start(bf16[3,24,128]{2,1,0:T(8,128)(2,1)S(1)} %get-tuple-element.25), channel_id=1, source_target_pairs={{0,1},{1,0},{4,5},{5,4},{8,9},{9,8},{12,13},{13,12},{2,3},{3,2},{6... | collective-permute-start | bytes 55304 | tf_op jit(solution)/shard_map/ppermute | solution.py:561
  6.8 1.8 %collective-permute-start.4 = (bf16[3,24,128]{2,1,0:T(8,128)(2,1)S(1)}, bf16[3,24,128]{2,1,0:T(8,128)(2,1)S(1)}, u32[]{:S(2)}, u32[]{:S(2)}) collective-permute-start(bf16[3,24,128]{2,1,0:T(8,128)(2,1)S(1)} %get-tuple-element.26), channel_id=1, source_target_pairs={{0,5},{1,4},{4,9},{5,8},{8,13},{9,12},{12,1},{13,0},{2,7},{3,6},{6... | collective-permute-start | bytes 55304 | tf_op jit(solution)/shard_map/ppermute | solution.py:561
  8.6 2.5 %collective-permute-start.5 = (bf16[3,24,128]{2,1,0:T(8,128)(2,1)S(1)}, bf16[3,24,128]{2,1,0:T(8,128)(2,1)S(1)}, u32[]{:S(2)}, u32[]{:S(2)}) collective-permute-start(bf16[3,24,128]{2,1,0:T(8,128)(2,1)S(1)} %get-tuple-element.27), channel_id=1, source_target_pairs={{0,9},{1,8},{4,13},{5,12},{8,1},{9,0},{12,5},{13,4},{2,11},{3,10},... | collective-permute-start | bytes 55304 | tf_op jit(solution)/shard_map/ppermute | solution.py:561
  11.1 1.1 %collective-permute-start.6 = (bf16[3,24,128]{2,1,0:T(8,128)(2,1)S(1)}, bf16[3,24,128]{2,1,0:T(8,128)(2,1)S(1)}, u32[]{:S(2)}, u32[]{:S(2)}) collective-permute-start(bf16[3,24,128]{2,1,0:T(8,128)(2,1)S(1)} %get-tuple-element.28), channel_id=1, source_target_pairs={{0,13},{1,12},{4,1},{5,0},{8,5},{9,4},{12,9},{13,8},{2,15},{3,14},... | collective-permute-start | bytes 55304 | tf_op jit(solution)/shard_map/ppermute | solution.py:561
  12.2 0.0 collective-permute-done.3.refs_0_
  12.2 0.0 collective-permute-done.4.refs_1_
  12.2 0.5 %collective-permute-done.5.refs_2_ = bf16[3,24,128]{2,1,0:T(8,128)(2,1)S(1)} collective-permute-done((bf16[3,24,128]{2,1,0:T(8,128)(2,1)S(1)}, bf16[3,24,128]{2,1,0:T(8,128)(2,1)S(1)}, u32[]{:S(2)}, u32[]{:S(2)}) %collective-permute-start.5) | collective-permute-done | bytes 18464 | tf_op jit(solution)/shard_map/ppermute | solution.py:561
  12.7 1.5 %collective-permute-done.6.refs_3_ = bf16[3,24,128]{2,1,0:T(8,128)(2,1)S(1)} collective-permute-done((bf16[3,24,128]{2,1,0:T(8,128)(2,1)S(1)}, bf16[3,24,128]{2,1,0:T(8,128)(2,1)S(1)}, u32[]{:S(2)}, u32[]{:S(2)}) %collective-permute-start.6) | collective-permute-done | bytes 18464 | tf_op jit(solution)/shard_map/ppermute | solution.py:561
  14.3 1.0 %shard_map.77 = bf16[1,1,3,4608]{3,2,1,0:T(4,128)(2,1)} custom-call(bf16[768,768]{1,0:T(8,128)(2,1)S(1)} %get-tuple-element.17.matrix, f32[8,256]{1,0:T(8,128)S(1)} %get-tuple-element.18.bias, s32[4,24,128]{2,1,0:T(8,128)S(1)} %get-tuple-element.19.picks, bf16[3,24,128]{2,1,0:T(8,128)(2,1)S(1)} %collective-permute-done.3.refs_0_, ...), custom_call_target="tpu_custom_call" | custom-call | flops 4194304 | bytes 1048576 | tf_op jit(solution)/shard_map/pallas_call | solution.py:570
Async XLA Ops:
  0.0 1.8 %collective-permute-start.1 = (bf16[1,8,4608]{2,1,0:T(8,128)(2,1)}, bf16[1,8,4608]{2,1,0:T(8,128)(2,1)S(1)}, u32[]{:S(2)}, u32[]{:S(2)}) collective-permute-start(bf16[1,8,4608]{2,1,0:T(8,128)(2,1)} %frames_far.1), channel_id=1, source_target_pairs={{0,1},{1,0},{2,3},{3,2},{4,5},{5,4},{6,7},{7,6},{8,9},{9,8},{10,11... | collective-permute-start | bytes 221192 | tf_op jit(solution)/shard_map/ppermute | solution.py:452
  0.5 1.3 %collective-permute-start = (s32[1,1,18]{2,1,0:T(1,128)}, s32[1,1,18]{2,1,0:T(1,128)S(1)}, u32[]{:S(2)}, u32[]{:S(2)}) collective-permute-start(s32[1,1,18]{2,1,0:T(1,128)} %valid_far.1), channel_id=1, source_target_pairs={{0,1},{1,0},{2,3},{3,2},{4,5},{5,4},{6,7},{7,6},{8,9},{9,8},{10,11... | collective-permute-start | bytes 224 | tf_op jit(solution)/shard_map/ppermute | solution.py:453
  1.9 4.3 %collective-permute-start.2 = (bf16[4,4736]{1,0:T(4,128)(2,1)S(1)}, bf16[4,4736]{1,0:T(4,128)(2,1)S(1)}, u32[]{:S(2)}, u32[]{:S(2)}) collective-permute-start(bf16[4,4736]{1,0:T(4,128)(2,1)S(1)} %shard_map.75), channel_id=1, source_target_pairs={{0,3},{1,2},{2,1},{3,0},{4,7},{5,6},{6,5},{7,4},{8,11},{9,10},{10,... | collective-permute-start | bytes 113672 | tf_op jit(solution)/shard_map/ppermute | solution.py:479
  6.5 5.7 %collective-permute-start.3 = (bf16[3,24,128]{2,1,0:T(8,128)(2,1)S(1)}, bf16[3,24,128]{2,1,0:T(8,128)(2,1)S(1)}, u32[]{:S(2)}, u32[]{:S(2)}) collective-permute-start(bf16[3,24,128]{2,1,0:T(8,128)(2,1)S(1)} %get-tuple-element.25), channel_id=1, source_target_pairs={{0,1},{1,0},{4,5},{5,4},{8,9},{9,8},{12,13},{13,12},{2,3},{3,2},{6... | collective-permute-start | bytes 55304 | tf_op jit(solution)/shard_map/ppermute | solution.py:561
  6.8 5.5 %collective-permute-start.4 = (bf16[3,24,128]{2,1,0:T(8,128)(2,1)S(1)}, bf16[3,24,128]{2,1,0:T(8,128)(2,1)S(1)}, u32[]{:S(2)}, u32[]{:S(2)}) collective-permute-start(bf16[3,24,128]{2,1,0:T(8,128)(2,1)S(1)} %get-tuple-element.26), channel_id=1, source_target_pairs={{0,5},{1,4},{4,9},{5,8},{8,13},{9,12},{12,1},{13,0},{2,7},{3,6},{6... | collective-permute-start | bytes 55304 | tf_op jit(solution)/shard_map/ppermute | solution.py:561
  8.6 4.2 %collective-permute-start.5 = (bf16[3,24,128]{2,1,0:T(8,128)(2,1)S(1)}, bf16[3,24,128]{2,1,0:T(8,128)(2,1)S(1)}, u32[]{:S(2)}, u32[]{:S(2)}) collective-permute-start(bf16[3,24,128]{2,1,0:T(8,128)(2,1)S(1)} %get-tuple-element.27), channel_id=1, source_target_pairs={{0,9},{1,8},{4,13},{5,12},{8,1},{9,0},{12,5},{13,4},{2,11},{3,10},... | collective-permute-start | bytes 55304 | tf_op jit(solution)/shard_map/ppermute | solution.py:561
  11.1 3.2 %collective-permute-start.6 = (bf16[3,24,128]{2,1,0:T(8,128)(2,1)S(1)}, bf16[3,24,128]{2,1,0:T(8,128)(2,1)S(1)}, u32[]{:S(2)}, u32[]{:S(2)}) collective-permute-start(bf16[3,24,128]{2,1,0:T(8,128)(2,1)S(1)} %get-tuple-element.28), channel_id=1, source_target_pairs={{0,13},{1,12},{4,1},{5,0},{8,5},{9,4},{12,9},{13,8},{2,15},{3,14},... | collective-permute-start | bytes 55304 | tf_op jit(solution)/shard_map/ppermute | solution.py:561
